TPU v7x, 512 devices: a whole 4x4x16 slice. The times are simulated.
512 devices in a mesh: row: 32 (over z, y_hi), col: 16 (over y_lo, x, core).
Axes of the slice: x: 4, y: 4 (y_hi: 2, y_lo: 2; y = y_hi * 2 + y_lo), z: 16, core: 2. Of those that a mesh axis runs over, the one named last changes fastest.
Arguments:
- z_trunk: bfloat16 [2048, 2048, 128], P('row', 'col'), may hold values from -6 to 6
- chain_id: int32 [2048], replicated, may hold values from 0 to 5, never falling along the last dimension, each value on 1 to 512 neighbouring positions
- residue: int32 [2048], replicated, may hold values from 0 to 47
- single: bfloat16 [2048, 768], P(('row', 'col')), may hold values from -6 to 6
- gain_single: float32 [768], replicated, may hold values from 0.1 to 1.9
- w_proj: bfloat16 [768, 3072], P(None, ('row', 'col')), may hold values from -8 to 8
- w_out: bfloat16 [768, 768], replicated, may hold values from -0.21875 to 0.21875
- gain_trunk: float32 [128], replicated, may hold values from 0.1 to 1.9
- w_pair: bfloat16 [128, 128], replicated, may hold values from -0.5 to 0.5
- rel_table: bfloat16 [71, 128], replicated, may hold values from -5 to 5
- gain_trans: float32 [2, 128], replicated, may hold values from 0.1 to 1.9
- w_up: bfloat16 [2, 128, 512], replicated, may hold values from -0.5 to 0.5
- w_down: bfloat16 [2, 256, 128], replicated, may hold values from -0.375 to 0.375
- gain_bias: float32 [128], replicated, may hold values from 0.1 to 1.9
- w_bias: bfloat16 [128, 16], replicated, may hold values from -2 to 2
Outputs:
- update: bfloat16 [2048, 768], P(('row', 'col'))
Inputs may be any that keep to these rules, and one draw needn't show every extreme that they name: `chain_id`: chain numbers never fall along the tokens.
All inputs are finite; a program needn't handle non-finite values.
Results may differ from a plain program's by a relative error of at most 0.039.
Values may be sent and summed in bfloat16 or wider, within the bound.
A program may use at most 64 MiB of HBM per device.

v0:
```python
import jax
import jax.numpy as jnp
from jax import lax
from jax.sharding import PartitionSpec as P

RMAX = 32
CMAX = 2


def joined(value, axis, join):
    pieces = jax.tree.map(lambda part: lax.all_gather(part, axis), value)
    head = jax.tree.map(lambda part: part[0], pieces)
    tail = jax.tree.map(lambda part: part[1:], pieces)
    total, _ = lax.scan(lambda total, share: (join(total, share), None), head, tail)
    return total


def layer_norm(values, gain):
    values = values.astype(jnp.float32)
    center = values - jnp.mean(values, axis=-1, keepdims=True)
    spread = jnp.mean(center * center, axis=-1, keepdims=True)
    return center * lax.rsqrt(spread + 1e-05) * gain


def pair_bias(
    pair_in,
    chain_q,
    res_q,
    chain_k,
    res_k,
    gain_trunk,
    w_pair,
    rel_table,
    gain_trans,
    w_up,
    w_down,
    gain_bias,
    w_bias,
):
    same_chain = chain_q[:, None] == chain_k[None, :]
    res_bin = jnp.where(
        same_chain, jnp.clip(res_q[:, None] - res_k[None, :], -RMAX, RMAX) + RMAX, 2 * RMAX + 1
    )
    chain_bin = jnp.clip(chain_q[:, None] - chain_k[None, :], -CMAX, CMAX) + 2 * RMAX + 2
    bins = jnp.arange(rel_table.shape[0], dtype=jnp.int32)
    one_hot = ((res_bin[..., None] == bins) | (chain_bin[..., None] == bins)).astype(jnp.bfloat16)
    width = pair_in.shape[-1]
    flat = pair_in.reshape(-1, width)
    one_hot = one_hot.reshape(flat.shape[0], -1)
    normed = layer_norm(flat, gain_trunk).astype(jnp.bfloat16)
    pair = (
        jnp.dot(normed, w_pair, preferred_element_type=jnp.float32)
        + jnp.dot(one_hot, rel_table, preferred_element_type=jnp.float32)
    ).astype(jnp.bfloat16)
    hidden = w_down.shape[1]
    for layer in range(w_up.shape[0]):
        normed = layer_norm(pair, gain_trans[layer]).astype(jnp.bfloat16)
        expanded = jnp.dot(normed, w_up[layer], preferred_element_type=jnp.float32)
        swiglu = (jax.nn.silu(expanded[:, :hidden]) * expanded[:, hidden:]).astype(jnp.bfloat16)
        pair = (
            pair.astype(jnp.float32)
            + jnp.dot(swiglu, w_down[layer], preferred_element_type=jnp.float32)
        ).astype(jnp.bfloat16)
    bias_normed = layer_norm(pair, gain_bias).astype(jnp.bfloat16)
    bias = jnp.dot(bias_normed, w_bias, preferred_element_type=jnp.float32)
    return bias.reshape(pair_in.shape[0], pair_in.shape[1], -1)


def shards(
    z_trunk,
    chain_id,
    residue,
    single,
    gain_single,
    w_proj,
    w_out,
    gain_trunk,
    w_pair,
    rel_table,
    gain_trans,
    w_up,
    w_down,
    gain_bias,
    w_bias,
):
    row_pos = lax.axis_index("row")
    col_pos = lax.axis_index("col")
    q_rows = z_trunk.shape[0]
    k_cols = z_trunk.shape[1]
    owned = single.shape[0]
    width = single.shape[1]
    heads = w_bias.shape[1]
    head_dim = width // heads
    normed = layer_norm(single, gain_single).astype(jnp.bfloat16)
    projected = jnp.dot(
        normed,
        lax.all_gather(w_proj, ("row", "col"), axis=1, tiled=True),
        preferred_element_type=jnp.float32,
    )
    queries = projected[:, :width].astype(jnp.bfloat16)
    keys_own = projected[:, width : 2 * width].astype(jnp.bfloat16)
    values_own = projected[:, 2 * width : 3 * width].astype(jnp.bfloat16)
    gating = jax.nn.sigmoid(projected[:, 3 * width :])
    chain_q = lax.dynamic_slice_in_dim(chain_id, row_pos * q_rows, q_rows, 0)
    res_q = lax.dynamic_slice_in_dim(residue, row_pos * q_rows, q_rows, 0)
    chain_k = lax.dynamic_slice_in_dim(chain_id, col_pos * k_cols, k_cols, 0)
    res_k = lax.dynamic_slice_in_dim(residue, col_pos * k_cols, k_cols, 0)
    block_rows = 8
    count_blocks = q_rows // block_rows

    def bias_block(inputs):
        pair_blk, chain_blk, res_blk = inputs
        return pair_bias(
            pair_blk,
            chain_blk,
            res_blk,
            chain_k,
            res_k,
            gain_trunk,
            w_pair,
            rel_table,
            gain_trans,
            w_up,
            w_down,
            gain_bias,
            w_bias,
        )

    bias = lax.map(
        bias_block,
        (
            z_trunk.reshape(count_blocks, block_rows, k_cols, -1),
            chain_q.reshape(count_blocks, block_rows),
            res_q.reshape(count_blocks, block_rows),
        ),
    )
    bias = jnp.transpose(bias.reshape(q_rows, k_cols, heads), (2, 0, 1))
    query_tile = lax.all_gather(queries, "col", axis=0, tiled=True)
    keys_all, values_all = (
        lax.all_gather(keys_own, ("row", "col"), axis=0, tiled=True),
        lax.all_gather(values_own, ("row", "col"), axis=0, tiled=True),
    )
    key_tile = lax.dynamic_slice_in_dim(keys_all, col_pos * k_cols, k_cols, 0)
    value_tile = lax.dynamic_slice_in_dim(values_all, col_pos * k_cols, k_cols, 0)
    query3 = query_tile.reshape(q_rows, heads, head_dim)
    key3 = key_tile.reshape(k_cols, heads, head_dim)
    value3 = value_tile.reshape(k_cols, heads, head_dim)
    scores = (
        jnp.einsum("qhd,khd->hqk", query3, key3, preferred_element_type=jnp.float32)
        / jnp.sqrt(jnp.float32(head_dim))
        + bias
    )
    local_max = jnp.max(scores, axis=-1)
    expo = jnp.exp(scores - local_max[:, :, None])
    totals = jnp.transpose(jnp.sum(expo, axis=-1))
    weights = expo.astype(jnp.bfloat16)
    weighted = jnp.einsum(
        "hqk,khd->qhd", weights, value3, preferred_element_type=jnp.float32
    ).reshape(q_rows, width)
    local_max = jnp.transpose(local_max)

    def rescale(summed, factor):
        rows = summed.shape[0]
        return (summed.reshape(rows, heads, head_dim) * factor[:, :, None]).reshape(rows, width)

    def join(first, second):
        peak = jnp.maximum(first[0], second[0])
        left = jnp.exp(first[0] - peak)
        right = jnp.exp(second[0] - peak)
        return (
            peak,
            first[1] * left + second[1] * right,
            rescale(first[2], left) + rescale(second[2], right),
        )

    merged_max, merged_totals, merged_sum = joined((local_max, totals, weighted), "col", join)
    own_totals = lax.dynamic_slice_in_dim(merged_totals, col_pos * owned, owned, 0)
    own_sum = lax.dynamic_slice_in_dim(merged_sum, col_pos * owned, owned, 0)
    attended = (rescale(own_sum, 1.0 / own_totals) * gating).astype(jnp.bfloat16)
    return jnp.dot(attended, w_out, preferred_element_type=jnp.float32).astype(jnp.bfloat16)


def solution(mesh):
    return jax.shard_map(
        shards,
        mesh=mesh,
        in_specs=(
            P("row", "col", None),
            P(),
            P(),
            P(("row", "col"), None),
            P(),
            P(None, ("row", "col")),
            P(),
            P(),
            P(),
            P(),
            P(),
            P(),
            P(),
            P(),
            P(),
        ),
        out_specs=P(("row", "col"), None),
        check_vma=False,
    )
```

profile of v0, /device:TPU:1, one launch (start us, length us, event | category | flops | bytes accessed | tf_op | source)
XLA Modules:
  0.0 711.8 jit_solution(6318479706813883494)
XLA Ops:
  9.0 208.5 %all-gather.15.cloned.1.call-done = bf16[512,6,768]{2,1,0:T(8,128)(2,1)} async-done(((bf16[1,6,768]{2,1,0:T(8,128)(2,1)}), bf16[512,6,768]{2,1,0:T(8,128)(2,1)}) %all-gather.15.cloned.1.call-update) | async-done | bytes 4718608 | tf_op jit(solution)/shard_map/all_gather | solution.py:97
  217.6 8.7 %reshape.265 = bf16[3072,768]{1,0:T(8,128)(2,1)} reshape(bf16[512,6,768]{2,1,0:T(8,128)(2,1)} %all-gather.15.cloned.1.call-done) | data formatting | bytes 9437184
  226.3 3.8 fusion.77
  234.2 66.0 %while.26 = (s32[]{:T(128)}, f32[8,8,128,16]{2,1,0,3:T(8,128)S(1)}, bf16[8,8,128,128]{3,2,1,0:T(8,128)(2,1)}, f32[128]{0:T(128)S(1)}, bf16[128,128]{1,0:T(8,128)...) while((s32[]{:T(128)}, f32[8,8,128,16]{2,1,0,3:T(8,128)S(1)}, ...), condition=%wide.region_11.12_spmd, body=%wide.region_2.11_spmd.sunk | while | flops 468157440 | bytes 17480816 | solution.py:129
  238.3 1.5 fusion.117
  243.5 1.3 multiply_reduce_fusion.8
  246.6 1.5 fusion.117
  254.8 1.5 fusion.117
  263.1 1.5 fusion.117
  268.3 1.3 multiply_reduce_fusion.8
  271.3 1.5 fusion.117
  279.6 1.5 fusion.117
  287.8 1.5 fusion.117
  296.1 1.5 fusion.117
  300.2 20.2 %all-gather.3 = bf16[16,4,768]{2,1,0:T(4,128)(2,1)S(1)} all-gather(bf16[1,4,768]{2,1,0:T(4,128)(2,1)S(1)} %get-tuple-element.304), channel_id=1, replica_groups=mesh['row'=32,'col'=16] {'col'}, dimensions={0}, use_global_device_ids=true | all-gather | bytes 104448 | tf_op jit(solution)/shard_map/all_gather | solution.py:138
  320.7 102.8 %all-gather.19.cloned.1.call-done = bf16[512,4,768]{2,1,0:T(4,128)(2,1)} async-done(((bf16[1,4,768]{2,1,0:T(4,128)(2,1)}), bf16[512,4,768]{2,1,0:T(4,128)(2,1)}) %all-gather.19.cloned.1.call-update) | async-done | bytes 3145744 | tf_op jit(solution)/shard_map/all_gather | solution.py:141
  423.5 6.0 reshape.275
  429.5 190.4 %all-gather.17.cloned.1.call-done = bf16[512,4,768]{2,1,0:T(4,128)(2,1)} async-done(((bf16[1,4,768]{2,1,0:T(4,128)(2,1)}), bf16[512,4,768]{2,1,0:T(4,128)(2,1)}) %all-gather.17.cloned.1.call-update) | async-done | bytes 3145744 | tf_op jit(solution)/shard_map/all_gather | solution.py:140
  619.9 5.9 reshape.269
  628.8 20.3 %all-gather.5 = f32[16,64,16]{1,2,0:T(8,128)S(1)} all-gather(f32[1,64,16]{1,2,0:T(8,128)S(1)} %bitcast.168), channel_id=2, replica_groups=mesh['row'=32,'col'=16] {'col'}, dimensions={0}, use_global_device_ids=true | all-gather | bytes 69632 | tf_op jit(solution)/shard_map/all_gather | solution.py:11
  649.6 16.6 %all-gather.6 = f32[16,64,16]{1,2,0:T(8,128)S(1)} all-gather(f32[1,64,16]{1,2,0:T(8,128)S(1)} %bitcast.169), channel_id=3, replica_groups=mesh['row'=32,'col'=16] {'col'}, dimensions={0}, use_global_device_ids=true | all-gather | bytes 69632 | tf_op jit(solution)/shard_map/all_gather | solution.py:11
  666.3 1.5 all-gather.13.cloned.1.call-done
  668.8 3.7 slice.123
  672.5 31.7 %while.27 = (s32[]{:T(128)}, f32[64,16]{1,0:T(8,128)S(1)}, f32[64,16]{1,0:T(8,128)S(1)}, f32[64,768]{1,0:T(8,128)S(1)}, f32[15,64,16]{1,2,0:T(8,128)S(1)}, /*ind...) while((s32[]{:T(128)}, f32[64,16]{1,0:T(8,128)S(1)}, f32[64,16]{1,0:T(8,128)S(1)}, ...), condition=%wide.region_15.16_spmd, body=%wide.region_14.15_spmd.sunk | while | flops 153602 | bytes 2236517 | solution.py:14
  (410 shorter events, 93.3 us)
Async XLA Ops:
  6.5 697.9 %copy-start = (bf16[768,768]{1,0:T(8,128)(2,1)S(1)}, bf16[768,768]{1,0:T(8,128)(2,1)}, u32[]{:S(2)}) copy-start(bf16[768,768]{1,0:T(8,128)(2,1)} %param.25) | copy-start | bytes 3538948
  6.5 211.0 %all-gather.15.cloned.1.call-start = ((), (), s32[]{:S(2)}) async-start(), calls=%async_computation.1 | async-start | bytes 6303744 | tf_op jit(solution)/shard_map/all_gather | solution.py:97
  7.3 416.3 %all-gather.19.cloned.1.call-start = ((), (), s32[]{:S(2)}) async-start(), calls=%async_computation.3 | async-start | bytes 3151872 | tf_op jit(solution)/shard_map/all_gather | solution.py:141
  9.0 217.2 %copy-start.5 = (bf16[4,768]{1,0:T(4,128)(2,1)S(1)}, bf16[4,768]{1,0:T(4,128)(2,1)}, u32[]{:S(2)}) copy-start(bf16[4,768]{1,0:T(4,128)(2,1)} %param.22) | copy-start | bytes 18436
  9.0 217.2 %copy-start.9 = (f32[768]{0:T(1024)S(1)}, f32[768]{0:T(1024)}, u32[]{:S(2)}) copy-start(f32[768]{0:T(1024)} %param.23) | copy-start | bytes 9220
  226.2 7.9 %copy-start.1 = (bf16[2,128,512]{2,1,0:T(8,128)(2,1)S(1)}, bf16[2,128,512]{2,1,0:T(8,128)(2,1)}, u32[]{:S(2)}) copy-start(bf16[2,128,512]{2,1,0:T(8,128)(2,1)} %param.30) | copy-start | bytes 786436
  226.2 7.9 %copy-start.2 = (bf16[128,128]{1,0:T(8,128)(2,1)S(1)}, bf16[128,128]{1,0:T(8,128)(2,1)}, u32[]{:S(2)}) copy-start(bf16[128,128]{1,0:T(8,128)(2,1)} %param.27) | copy-start | bytes 98308
  226.2 7.9 %copy-start.3 = (bf16[71,128]{1,0:T(8,128)(2,1)S(1)}, bf16[71,128]{1,0:T(8,128)(2,1)}, u32[]{:S(2)}) copy-start(bf16[71,128]{1,0:T(8,128)(2,1)} %param.28) | copy-start | bytes 54532
  226.3 7.9 %copy-start.4 = (bf16[128,16]{0,1:T(8,128)(2,1)S(1)}, bf16[128,16]{0,1:T(8,128)(2,1)}, u32[]{:S(2)}) copy-start(bf16[128,16]{0,1:T(8,128)(2,1)} %param.33) | copy-start | bytes 12292
  226.3 7.9 %copy-start.6 = (f32[2,128]{1,0:T(2,128)S(1)}, f32[2,128]{1,0:T(2,128)}, u32[]{:S(2)}) copy-start(f32[2,128]{1,0:T(2,128)} %param.29) | copy-start | bytes 3076
  226.3 7.9 %copy-start.7 = (f32[128]{0:T(128)S(1)}, f32[128]{0:T(128)}, u32[]{:S(2)}) copy-start(f32[128]{0:T(128)} %param.26) | copy-start | bytes 1540
  226.3 7.9 %copy-start.8 = (f32[128]{0:T(128)S(1)}, f32[128]{0:T(128)}, u32[]{:S(2)}) copy-start(f32[128]{0:T(128)} %param.32) | copy-start | bytes 1540
  226.3 7.9 %copy-start.10 = (bf16[2,256,128]{2,1,0:T(8,128)(2,1)S(1)}, bf16[2,256,128]{2,1,0:T(8,128)(2,1)}, u32[]{:S(2)}) copy-start(bf16[2,256,128]{2,1,0:T(8,128)(2,1)} %param.31) | copy-start | bytes 393220
  230.7 389.2 %all-gather.17.cloned.1.call-start = ((), (), s32[]{:S(2)}) async-start(), calls=%async_computation.2 | async-start | bytes 3151872 | tf_op jit(solution)/shard_map/all_gather | solution.py:140
  234.0 433.8 %all-gather.13.cloned.1.call-start = ((), (), s32[]{:S(2)}) async-start(), calls=%async_computation | async-start | bytes 3342336 | tf_op jit(solution)/shard_map/all_gather | solution.py:11
Sparse Core Ops, SparseCore 0:
  11.7 205.7 all-gather.14
  230.8 192.6 all-gather.18
  427.9 191.9 all-gather.16
  628.9 38.8 all-gather.12
where the time goes:
time: 714 us; the launch traced here: 712 us
  waiting for transfers between devices  504 us (71%)
  blocking collectives  57.1 us (8%)
  other arithmetic  50 us (7%)
  local copies, waits for them, and re-layouts  47.8 us (7%)
  matrix products  37.2 us (5%)
  between operations  13.4 us (2%)
    all_gather x1, waiting for transfers between devices, shards(): lax.all_gather(w_proj, ('row', 'col'), axis=1, tiled=True)  209 us
    all_gather x1, waiting for transfers between devices, shards(): lax.all_gather(keys_own, ('row', 'col'), axis=0, tiled=True)  190 us
    all_gather x1, waiting for transfers between devices, shards(): lax.all_gather(values_own, ('row', 'col'), axis=0, tiled=True)  103 us
    all_gather x2, blocking collectives, joined(): pieces = jax.tree.map(lambda part: lax.all_gather(part, axis), value)  36.9 us
    unnamed x28, local copies, waits for them, and re-layouts  21.6 us
    all_gather x1, blocking collectives, shards(): query_tile = lax.all_gather(queries, 'col', axis=0, tiled=True)  20.2 us
    add x15, other arithmetic, join(): rescale(first[2], left) + rescale(second[2], right)  15 us
  transfers between devices with their start and end apart: 4, of which 4 were waited for; matrix products, arithmetic and copies ran while one was open for 11% of the time, Pallas kernels for 0%

commit v1 on v0

v1 whole, which is shorter than its diff:
```python
import functools

import jax
import jax.numpy as jnp
import numpy as np
from jax import lax
from jax.experimental import pallas as pl
from jax.experimental.pallas import tpu as pltpu
from jax.sharding import PartitionSpec as P

NT = (((1,), (1,)), ((), ()))
F32 = jnp.float32
BF16 = jnp.bfloat16
BIG = 1 << 20
QB = 32


def norm_cols(values):
    center = values - jnp.mean(values, axis=0, keepdims=True)
    spread = jnp.mean(center * center, axis=0, keepdims=True)
    return (center * lax.rsqrt(spread + 1e-05)).astype(BF16)


def interval_bounds(chain_k, res_k):
    bins = lax.broadcasted_iota(jnp.int32, (128, 128), 0)
    base = jnp.broadcast_to(chain_k * 64, (128, 128))
    res = jnp.broadcast_to(res_k, (128, 128))
    shifted = res + bins - 32
    inside = (shifted >= 0) & (shifted <= 63)
    low = jnp.where(inside, base + shifted, BIG)
    high = jnp.where(inside, base + shifted, -BIG)

    def put(low, high, index, new_low, new_high):
        hit = bins == index
        return jnp.where(hit, new_low, low), jnp.where(hit, new_high, high)

    low, high = put(low, high, 0, base, base + res - 32)
    low, high = put(low, high, 64, base + res + 32, base + 63)
    low, high = put(low, high, 65, jnp.full_like(base, -BIG), base - 1)
    low, high = put(low, high, 66, base, base + 63)
    low, high = put(low, high, 67, base + 64, base + 127)
    low, high = put(low, high, 68, base + 128, jnp.full_like(base, BIG))
    low, high = put(low, high, 69, jnp.full_like(base, -BIG), base - 65)
    low, high = put(low, high, 70, base + 64, jnp.full_like(base, BIG))
    unused = bins > 70
    return jnp.where(unused, BIG, low), jnp.where(unused, -BIG, high)


def bias_kernel(
    chain_sm, res_sm, z_ref, chain_ref, res_ref, gtrunk_ref, wpair_ref, rel_ref, gtrans_ref,
    wup_ref, wdown_ref, gbias_ref, wbias_ref, out_ref, low_ref, high_ref, wcat, wup, wdn, wb, rel,
):
    step = pl.program_id(0)
    row_pos = lax.axis_index("row")
    col_pos = lax.axis_index("col")

    @pl.when(step == 0)
    def _():
        low, high = interval_bounds(chain_ref[pl.ds(col_pos, 1), :], res_ref[pl.ds(col_pos, 1), :])
        low_ref[...] = low
        high_ref[...] = high
        wcat[:, :128] = (wpair_ref[...].astype(F32).T * gtrunk_ref[...]).astype(BF16)
        rel[...] = jnp.zeros_like(rel)
        rel[0:69, :] = rel_ref[0:69, :].astype(F32)
        rel[69:70, :] = rel_ref[64:65, :].astype(F32)
        rel[70:71, :] = rel_ref[65:66, :].astype(F32)
        wcat[:, 128:] = rel[...].T.astype(BF16)
        for t in range(2):
            up = wup_ref[t].astype(F32).T * gtrans_ref[t : t + 1, :]
            wup[t, :256] = (up[:256] * 0.5).astype(BF16)
            wup[t, 256:] = up[256:].astype(BF16)
            wdn[t] = wdown_ref[t].astype(F32).T.astype(BF16)
        wb[...] = (wbias_ref[...].astype(F32).T * gbias_ref[...]).astype(BF16)

    low = low_ref[...]
    high = high_ref[...]
    tiles = [z_ref[j].astype(F32).T for j in range(QB)]
    normed = norm_cols(jnp.concatenate(tiles, axis=1))
    hots = []
    for j in range(QB):
        token = row_pos * 64 + step * QB + j
        code = chain_sm[token] * 64 + res_sm[token]
        hots.append(jnp.where((low <= code) & (high >= code), 1.0, 0.0).astype(BF16))
    both = jnp.concatenate([normed, jnp.concatenate(hots, axis=1)], axis=0)
    pair = jnp.dot(wcat[...], both, preferred_element_type=F32)
    for t in range(2):
        expanded = jnp.dot(wup[t], norm_cols(pair), preferred_element_type=F32)
        half = expanded[:256]
        product = half * expanded[256:]
        swiglu = (product + product * jnp.tanh(half)).astype(BF16)
        pair = pair + jnp.dot(wdn[t], swiglu, preferred_element_type=F32)
    bias = jnp.dot(wb[...], norm_cols(pair), preferred_element_type=F32)
    for j in range(QB):
        out_ref[j] = bias[:, j * 128 : (j + 1) * 128]


def pair_bias(z, chain_id, residue, gain_trunk, w_pair, rel_table, gain_trans, w_up, w_down, gain_bias, w_bias):
    def full(*shape):
        return pl.BlockSpec(shape, lambda i, *_: (0,) * len(shape))

    spec = pltpu.PrefetchScalarGridSpec(
        num_scalar_prefetch=2,
        grid=(64 // QB,),
        in_specs=[
            pl.BlockSpec((QB, 128, 128), lambda i, *_: (i, 0, 0)),
            full(16, 128), full(16, 128), full(1, 128), full(128, 128), full(71, 128), full(2, 128),
            full(2, 128, 512), full(2, 256, 128), full(1, 128), full(128, 16),
        ],
        out_specs=pl.BlockSpec((QB, 16, 128), lambda i, *_: (i, 0, 0)),
        scratch_shapes=[
            pltpu.VMEM((128, 128), jnp.int32),
            pltpu.VMEM((128, 128), jnp.int32),
            pltpu.VMEM((128, 256), BF16),
            pltpu.VMEM((2, 512, 128), BF16),
            pltpu.VMEM((2, 128, 256), BF16),
            pltpu.VMEM((16, 128), BF16),
            pltpu.VMEM((128, 128), F32),
        ],
    )
    return pl.pallas_call(
        bias_kernel,
        grid_spec=spec,
        out_shape=jax.ShapeDtypeStruct((64, 16, 128), F32),
        compiler_params=pltpu.CompilerParams(vmem_limit_bytes=60 << 20),
    )(
        chain_id, residue, z, chain_id.reshape(16, 128), residue.reshape(16, 128), gain_trunk.reshape(1, 128),
        w_pair, rel_table, gain_trans, w_up, w_down, gain_bias.reshape(1, 128), w_bias,
    )


def orders():
    natural = np.zeros(768, np.int64)
    for g in range(32):
        for zk in range(4):
            for i in range(6):
                natural[g * 24 + zk * 6 + i] = 192 * zk + 6 * g + i
    heads = np.zeros((128, 768), np.float32)
    heads[natural // 48, np.arange(768)] = 1.0
    perm = np.zeros((768, 768), np.float32)
    perm[np.arange(768), natural] = 1.0
    return heads, perm


def main_kernel(
    x_ref, gain_ref, wt_ref, heads_ref, bias_hbm, wout_hbm, perm_hbm, out_ref,
    xs, xg, wg, xf, wf, kvs, qgs, kvz, kvb, qgb, tf, kt, vt, qf, gate, bias, wout, perm, woutp,
    o_src, o_all, st_src, st_all, fac,
    local_sem, w_send, w_recv, x_send, x_recv, qg_send, qg_recv, kz_send, kz_recv, kv_send, kv_recv,
    o_send, o_recv, st_send, st_recv,
):
    row_pos = lax.axis_index("row")
    col_pos = lax.axis_index("col")
    z = lax.div(row_pos, 2)
    yh = lax.rem(row_pos, 2)
    g = yh * 16 + col_pos

    def line(zz):
        return {"row": zz * 2 + yh, "col": col_pos}

    def plane(gg):
        return {"row": z * 2 + lax.div(gg, 16), "col": lax.rem(gg, 16)}

    def remote(src, dst, send, recv, device):
        return pltpu.make_async_remote_copy(
            src_ref=src, dst_ref=dst, send_sem=send, recv_sem=recv,
            device_id=device, device_id_type=pl.DeviceIdType.MESH,
        )

    def wait(ref, sem):
        pltpu.make_async_copy(ref, ref, sem).wait()

    def loop(count, body):
        lax.fori_loop(0, count, lambda i, carry: (body(i), carry)[1], 0)

    def far(i):
        return 8 + lax.div(i + 1, 2) * (1 - 2 * lax.rem(i, 2))

    def near(i):
        return lax.rem(16 + lax.div(i + 1, 2) * (1 - 2 * lax.rem(i, 2)), 16)

    loads = [
        pltpu.make_async_copy(bias_hbm, bias, local_sem.at[0]),
        pltpu.make_async_copy(wout_hbm, wout, local_sem.at[1]),
        pltpu.make_async_copy(perm_hbm, perm, local_sem.at[2]),
    ]
    barrier = pltpu.get_barrier_semaphore()

    def greet_line(i):
        pl.semaphore_signal(barrier, inc=1, device_id=line(lax.rem(z + 1 + i, 16)), device_id_type=pl.DeviceIdType.MESH)

    def greet_plane(i):
        pl.semaphore_signal(barrier, inc=1, device_id=plane(lax.rem(g + 1 + i, 32)), device_id_type=pl.DeviceIdType.MESH)

    loop(15, greet_line)
    loop(31, greet_plane)
    for load in loads:
        load.start()
    x = x_ref[...].astype(F32)
    center = x - jnp.mean(x, axis=-1, keepdims=True)
    spread = jnp.mean(center * center, axis=-1, keepdims=True)
    xs[...] = (center * lax.rsqrt(spread + 1e-05) * gain_ref[...]).astype(BF16)
    pl.semaphore_wait(barrier, 46)

    loop(15, lambda i: remote(wt_ref, wg.at[z], w_send, w_recv, line(lax.rem(z + far(i), 16))).start())
    loop(31, lambda i: remote(xs, xg.at[g], x_send, x_recv, plane(lax.rem(g + 1 + i, 32))).start())
    pltpu.make_async_copy(wt_ref, wg.at[z], w_recv).start()
    pltpu.make_async_copy(xs, xg.at[g], x_recv).start()
    wait(xg, x_recv)
    for s in range(32):
        xf[4 * s : 4 * s + 4, :] = xg[s].astype(F32)
    wait(wg, w_recv)
    for s in range(16):
        wf[6 * s : 6 * s + 6, :] = wg[s].astype(F32)
    projected = lax.dot_general(
        wf[...].astype(BF16), xf[...].astype(BF16), NT, preferred_element_type=F32
    )
    kvs[...] = projected[24:72].astype(BF16)
    qgs[0:24] = projected[0:24].astype(BF16)
    qgs[24:48] = jax.nn.sigmoid(projected[72:96]).astype(BF16)

    loop(15, lambda i: remote(kvs, kvz.at[z], kz_send, kz_recv.at[z], line(lax.rem(z + far(i), 16))).start())
    loop(31, lambda i: remote(qgs, qgb.at[g], qg_send, qg_recv, plane(lax.rem(g + 1 + i, 32))).start())
    pltpu.make_async_copy(qgs, qgb.at[g], qg_recv).start()
    pltpu.make_async_copy(kvs, kvz.at[z], kz_recv.at[z]).start()
    loads[1].wait()
    loads[2].wait()
    woutp[...] = jnp.dot(perm[...], wout[...], preferred_element_type=F32).astype(BF16)
    wait(qgb, qg_recv)

    def unpack(ref, first, dst):
        def body(s):
            dst[pl.ds(pl.multiple_of(s * 24, 8), 24), :] = ref[s, first : first + 24, :].astype(F32)

        loop(32, body)

    unpack(qgb, 0, tf)
    rows = lax.broadcasted_iota(jnp.int32, (64, 128), 0)
    lanes = lax.broadcasted_iota(jnp.int32, (64, 128), 1)
    pick = jnp.where(rows + yh * 64 == lanes, 1.0, 0.0).astype(BF16)
    qf[...] = lax.dot_general(pick, tf[...].astype(BF16), NT, preferred_element_type=F32)
    unpack(qgb, 24, tf)
    rows = lax.broadcasted_iota(jnp.int32, (8, 128), 0)
    lanes = lax.broadcasted_iota(jnp.int32, (8, 128), 1)
    pick = jnp.where((rows + yh * 64 + col_pos * 4 == lanes) & (rows < 4), 1.0, 0.0).astype(BF16)
    gate[...] = lax.dot_general(pick, tf[...].astype(BF16), NT, preferred_element_type=F32)

    def forward(i):
        s = lax.rem(z + near(i), 16)
        wait(kvz.at[s], kz_recv.at[s])
        for y in range(2):
            itself = (yh == y) & (col_pos == s)

            @pl.when(itself)
            def _():
                pltpu.make_async_copy(kvz.at[s], kvb.at[g], kv_recv).start()

            @pl.when(jnp.logical_not(itself))
            def _():
                remote(kvz.at[s], kvb.at[g], kv_send, kv_recv, {"row": z * 2 + y, "col": s}).start()

    loop(16, forward)
    loads[0].wait()
    wait(kvb, kv_recv)
    unpack(kvb, 0, tf)
    kt[...] = tf[...].astype(BF16)
    unpack(kvb, 24, tf)
    vt[...] = tf[...].astype(BF16)

    mask = heads_ref[0:16, :].astype(F32)
    rows = lax.broadcasted_iota(jnp.int32, (128, 128), 0)
    lanes = lax.broadcasted_iota(jnp.int32, (128, 128), 1)
    own = jnp.where(jnp.bitwise_and(rows, 15) == lanes, 1.0, 0.0)

    def send_parts(d):
        @pl.when(d == col_pos)
        def _():
            pltpu.make_async_copy(o_src.at[d], o_all.at[col_pos], o_recv).start()
            pltpu.make_async_copy(st_src.at[d], st_all.at[col_pos], st_recv).start()

        @pl.when(d != col_pos)
        def _():
            there = {"row": row_pos, "col": d}
            remote(o_src.at[d], o_all.at[col_pos], o_send, o_recv, there).start()
            remote(st_src.at[d], st_all.at[col_pos], st_send, st_recv, there).start()

    def attend(i):
        base = pl.multiple_of(i * 128, 128)
        queries = qf[pl.ds(pl.multiple_of(i * 8, 8), 8), :]
        spread_q = (queries[:, None, :] * mask[None]).reshape(128, 768).astype(BF16)
        scores = jnp.dot(spread_q, kt[...], preferred_element_type=F32) * (48.0**-0.5) + bias[pl.ds(base, 128), :]
        peak = jnp.max(scores, axis=-1, keepdims=True)
        expo = jnp.exp(scores - peak)
        total = jnp.sum(expo, axis=-1, keepdims=True)
        wide = lax.dot_general(expo.astype(BF16), vt[...], NT, preferred_element_type=F32)
        summed = jnp.sum(wide.reshape(8, 16, 768) * mask[None], axis=1).astype(BF16)
        peaks = jnp.sum((peak * own).reshape(8, 16, 128), axis=1)
        totals = jnp.sum((total * own).reshape(8, 16, 128), axis=1)
        for k in range(2):
            o_src[i * 2 + k] = summed[4 * k : 4 * k + 4]
            st_src[i * 2 + k, 0:4, :] = peaks[4 * k : 4 * k + 4]
            st_src[i * 2 + k, 4:8, :] = totals[4 * k : 4 * k + 4]

    loop(8, attend)
    loop(16, send_parts)
    wait(st_all, st_recv)
    stats = st_all[...]
    peak = stats[0, 0:4]
    for s in range(1, 16):
        peak = jnp.maximum(peak, stats[s, 0:4])
    factors = [jnp.exp(stats[s, 0:4] - peak) for s in range(16)]
    total = factors[0] * stats[0, 4:8]
    for s in range(1, 16):
        total = total + factors[s] * stats[s, 4:8]
    lanes = lax.broadcasted_iota(jnp.int32, (4, 128), 1)
    inverse = 1.0 / jnp.where(lanes < 16, total, 1.0)
    for s in range(16):
        fac[4 * s : 4 * s + 4, :] = jnp.where(lanes < 16, factors[s] * inverse, 0.0)
    coarse = fac[...].astype(BF16)
    fine = (fac[...] - coarse.astype(F32)).astype(BF16)
    wide = jnp.dot(coarse, heads_ref[...], preferred_element_type=F32) + jnp.dot(
        fine, heads_ref[...], preferred_element_type=F32
    )
    wait(o_all, o_recv)
    summed = wide[0:4] * o_all[0].astype(F32)
    for s in range(1, 16):
        summed = summed + wide[4 * s : 4 * s + 4] * o_all[s].astype(F32)
    attended = (summed * gate[0:4]).astype(BF16)
    out_ref[...] = jnp.dot(attended, woutp[...], preferred_element_type=F32).astype(BF16)

    wait(wg.at[pl.ds(0, 15)], w_send)
    wait(xg.at[pl.ds(0, 31)], x_send)
    wait(kvz.at[pl.ds(0, 15)], kz_send)
    wait(qgb.at[pl.ds(0, 31)], qg_send)
    wait(o_all.at[pl.ds(0, 15)], o_send)
    wait(st_all.at[pl.ds(0, 15)], st_send)
    wait(kvb.at[pl.ds(0, 31)], kv_send)


def shards(
    z_trunk, chain_id, residue, single, gain_single, w_proj, w_out, gain_trunk, w_pair, rel_table, gain_trans,
    w_up, w_down, gain_bias, w_bias,
):
    bias = pair_bias(
        z_trunk, chain_id, residue, gain_trunk, w_pair, rel_table, gain_trans, w_up, w_down, gain_bias, w_bias
    ).reshape(1024, 128)
    heads, perm = orders()
    vmem = pl.BlockSpec(memory_space=pltpu.VMEM)
    anywhere = pl.BlockSpec(memory_space=pl.ANY)
    dma = pltpu.SemaphoreType.DMA
    return pl.pallas_call(
        main_kernel,
        out_shape=jax.ShapeDtypeStruct((4, 768), BF16),
        in_specs=[vmem] * 4 + [anywhere] * 3,
        out_specs=vmem,
        scratch_shapes=[
            pltpu.VMEM((4, 768), BF16),
            pltpu.VMEM((32, 4, 768), BF16),
            pltpu.VMEM((16, 6, 768), BF16),
            pltpu.VMEM((128, 768), F32),
            pltpu.VMEM((96, 768), F32),
            pltpu.VMEM((48, 128), BF16),
            pltpu.VMEM((48, 128), BF16),
            pltpu.VMEM((16, 48, 128), BF16),
            pltpu.VMEM((32, 48, 128), BF16),
            pltpu.VMEM((32, 48, 128), BF16),
            pltpu.VMEM((768, 128), F32),
            pltpu.VMEM((768, 128), BF16),
            pltpu.VMEM((768, 128), BF16),
            pltpu.VMEM((64, 768), F32),
            pltpu.VMEM((8, 768), F32),
            pltpu.VMEM((1024, 128), F32),
            pltpu.VMEM((768, 768), BF16),
            pltpu.VMEM((768, 768), BF16),
            pltpu.VMEM((768, 768), BF16),
            pltpu.VMEM((16, 4, 768), BF16),
            pltpu.VMEM((16, 4, 768), BF16),
            pltpu.VMEM((16, 8, 128), F32),
            pltpu.VMEM((16, 8, 128), F32),
            pltpu.VMEM((64, 128), F32),
            dma((3,)),
            dma, dma, dma, dma, dma, dma, dma, dma((16,)), dma, dma, dma, dma, dma, dma,
        ],
        compiler_params=pltpu.CompilerParams(
            collective_id=0, has_side_effects=True, vmem_limit_bytes=40 << 20
        ),
    )(
        single, gain_single.reshape(1, 768), w_proj.T, jnp.asarray(heads, BF16), bias, w_out,
        jnp.asarray(perm, BF16),
    )


def solution(mesh):
    return jax.shard_map(
        shards,
        mesh=mesh,
        in_specs=(
            P("row", "col", None), P(), P(), P(("row", "col"), None), P(), P(None, ("row", "col")),
            P(), P(), P(), P(), P(), P(), P(), P(), P(),
        ),
        out_specs=P(("row", "col"), None),
        check_vma=False,
    )
```

time: 714 us -> 70.8 us (0.10)
  waiting for transfers between devices: 504 us -> 0 us
  Pallas kernels: 0 us -> 67.4 us
  blocking collectives: 57.1 us -> 0 us
  other arithmetic: 50 us -> 0 us
  local copies, waits for them, and re-layouts: 47.8 us -> 3.06 us
  matrix products: 37.2 us -> 0 us
  between operations: 13.4 us -> 0.08 us
    all_gather x4 -> x0, waiting for transfers between devices: 503 us -> none  [the longest x1 209 us: shards(): lax.all_gather(w_proj, ('row', 'col'), axis=1, tiled=True)]
    pallas_call x0 -> x2, Pallas kernels: none -> 67.4 us  [the longest x1 53.5 us: shards(): pl.pallas_call(main_kernel, out_shape=jax.ShapeDtypeStruct((4, 768), BF16...]
    all_gather x3 -> x0, blocking collectives: 57.1 us -> none  [the longest x2 36.9 us: joined(): pieces = jax.tree.map(lambda part: lax.all_gather(part, axis), value)]
    dot_general x60 -> x0, matrix products: 37.2 us -> none  [the longest x8 11.9 us: pair_bias(): jnp.dot(one_hot, rel_table, preferred_element_type=jnp.float32)]
    reduce_sum x43 -> x0, other arithmetic: 23.1 us -> none  [the longest x33 13.2 us: layer_norm(): spread = jnp.mean(center * center, axis=-1, keepdims=True)]
    unnamed x28 -> x16, local copies, waits for them, and re-layouts: 21.6 us -> 3.06 us
    add x30 -> x0, other arithmetic: 15.6 us -> none  [the longest x15 15 us: join(): rescale(first[2], left) + rescale(second[2], right)]
    mul x70 -> x0, local copies, waits for them, and re-layouts: 13 us -> none  [the longest x62 13 us: rescale(): summed.reshape(rows, heads, head_dim) * factor[:, :, None]]
  transfers between devices with their start and end apart: 4 -> 0, of which waited for: 4 -> 0; matrix products, arithmetic and copies ran while one was open for 11% -> 0% of each run, Pallas kernels for 0% -> 0%
where the time goes in v1:
time: 70.8 us; the launch traced here: 70.5 us
  Pallas kernels  67.4 us (95%)
  local copies, waits for them, and re-layouts  3.06 us (4%)
    pallas_call x1, Pallas kernels, shards(): pl.pallas_call(main_kernel, out_shape=jax.ShapeDtypeStruct((4, 768), BF16...  53.5 us
    pallas_call x1, Pallas kernels, pair_bias(): pl.pallas_call(bias_kernel, grid_spec=spec, out_shape=jax.ShapeDtypeStruc...  13.9 us
    unnamed x16, local copies, waits for them, and re-layouts  3.06 us

profile of v1, /device:TPU:1, one launch (start us, length us, event | category | flops | bytes accessed | tf_op | source)
XLA Modules:
  0.0 70.5 jit_solution(3063392516566759689)
XLA Ops:
  0.0 1.4 %copy.18.wbias_ref = bf16[128,16]{1,0:T(8,128)(2,1)} copy(bf16[128,16]{0,1:T(8,128)(2,1)} %param.31) | data formatting | bytes 8192 | tf_op args[14]
  1.4 0.0 copy-start.6
  1.4 0.0 copy-start.1
  1.4 0.0 copy-start.2
  1.4 0.0 copy-start.3
  1.4 0.0 copy-start.4
  1.4 0.0 copy-start.5
  1.4 13.9 %shard_map.163 = f32[64,16,128]{2,1,0:T(8,128)} custom-call(s32[2048]{0:T(1024)} %chain_sm.1, s32[2048]{0:T(1024)} %res_sm.1, bf16[64,128,128]{2,1,0:T(8,128)(2,1)} %z_ref.1, s32[16,128]{1,0:T(8,128)} %bitcast.8, s32[16,128]{1,0:T(8,128)} %bitcast.9, f32[1,128]{1,0:T(1,128)} %bitcast.10, bf16[128,128]{1,0:T(8,128)(2,1)} %wpair_ref.1, ...), custom_call_target="tpu_custom_call" | custom-call | tf_op jit(solution)/shard_map/pallas_call | solution.py:120
  15.3 0.0 copy-done.6
  15.3 0.0 copy-done.1
  15.3 0.0 copy-done.2
  15.4 0.0 copy-done.3
  15.4 0.0 copy-done.4
  15.4 0.0 copy-done.5
  15.4 0.0 copy-start
  15.4 1.0 %copy-done = f32[64,16,128]{2,1,0:T(8,128)S(1)} copy-done((f32[64,16,128]{2,1,0:T(8,128)S(1)}, f32[64,16,128]{2,1,0:T(8,128)}, u32[]{:S(2)}) %copy-start) | copy-done | bytes 524312
  16.4 53.5 %shard_map.164 = bf16[4,768]{1,0:T(4,128)(2,1)S(1)} custom-call(bf16[4,768]{1,0:T(4,128)(2,1)S(1)} %copy-done.5, f32[1,768]{1,0:T(1,128)S(1)} %reshape.18.gain_ref, bf16[6,768]{1,0:T(8,128)(2,1)S(1)} %bitcast.7, bf16[128,768]{1,0:T(8,128)(2,1)S(1)} %copy-done.3, f32[1024,128]{1,0:T(8,128)S(1)} %bitcast.6, bf16[768,768]{1,0:T(8,128)(2,1)S(1)} %copy-done.1, ...), custom_call_target="tpu_custom_call" | custom-call | tf_op jit(solution)/shard_map/pallas_call | solution.py:350
  69.9 0.6 copy.20
  (1 shorter events, 0.0 us)
Async XLA Ops:
  1.4 13.9 %copy-start.6 = (f32[768]{0:T(1024)S(1)}, f32[768]{0:T(1024)}, u32[]{:S(2)}) copy-start(f32[768]{0:T(1024)} %param.21) | copy-start | bytes 9220
  1.4 13.9 %copy-start.1 = (bf16[768,768]{1,0:T(8,128)(2,1)S(1)}, bf16[768,768]{1,0:T(8,128)(2,1)}, u32[]{:S(2)}) copy-start(bf16[768,768]{1,0:T(8,128)(2,1)} %wout_hbm.1) | copy-start | bytes 3538948
  1.4 13.9 %copy-start.2 = (bf16[768,768]{1,0:T(8,128)(2,1)S(1)}, bf16[768,768]{1,0:T(8,128)(2,1)}, u32[]{:S(2)}) copy-start(bf16[768,768]{1,0:T(8,128)(2,1)} %constant.5.clone.perm_hbm) | copy-start | bytes 3538948
  1.4 14.0 %copy-start.3 = (bf16[128,768]{1,0:T(8,128)(2,1)S(1)}, bf16[128,768]{1,0:T(8,128)(2,1)}, u32[]{:S(2)}) copy-start(bf16[128,768]{1,0:T(8,128)(2,1)} %constant.4.clone.heads_ref) | copy-start | bytes 589828
  1.4 14.0 %copy-start.4 = (bf16[768,6]{0,1:T(8,128)(2,1)S(1)}, bf16[768,6]{0,1:T(8,128)(2,1)}, u32[]{:S(2)}) copy-start(bf16[768,6]{0,1:T(8,128)(2,1)} %param.22) | copy-start | bytes 27652
  1.4 14.0 %copy-start.5 = (bf16[4,768]{1,0:T(4,128)(2,1)S(1)}, bf16[4,768]{1,0:T(4,128)(2,1)}, u32[]{:S(2)}) copy-start(bf16[4,768]{1,0:T(4,128)(2,1)} %x_ref.1) | copy-start | bytes 18436
  15.4 1.0 %copy-start = (f32[64,16,128]{2,1,0:T(8,128)S(1)}, f32[64,16,128]{2,1,0:T(8,128)}, u32[]{:S(2)}) copy-start(f32[64,16,128]{2,1,0:T(8,128)} %shard_map.163) | copy-start | bytes 1572868

commit v2 on v1

--- a/solution.py
+++ b/solution.py
@@ -12,7 +12,8 @@
 F32 = jnp.float32
 BF16 = jnp.bfloat16
 BIG = 1 << 20
-QB = 32
+QB = 16
+B0, B1, B2 = 1, 2, 1
 
 
 def norm_cols(values):
@@ -46,40 +47,35 @@
     return jnp.where(unused, BIG, low), jnp.where(unused, -BIG, high)
 
 
-def bias_kernel(
-    chain_sm, res_sm, z_ref, chain_ref, res_ref, gtrunk_ref, wpair_ref, rel_ref, gtrans_ref,
-    wup_ref, wdown_ref, gbias_ref, wbias_ref, out_ref, low_ref, high_ref, wcat, wup, wdn, wb, rel,
-):
-    step = pl.program_id(0)
-    row_pos = lax.axis_index("row")
-    col_pos = lax.axis_index("col")
-
-    @pl.when(step == 0)
-    def _():
-        low, high = interval_bounds(chain_ref[pl.ds(col_pos, 1), :], res_ref[pl.ds(col_pos, 1), :])
-        low_ref[...] = low
-        high_ref[...] = high
-        wcat[:, :128] = (wpair_ref[...].astype(F32).T * gtrunk_ref[...]).astype(BF16)
-        rel[...] = jnp.zeros_like(rel)
-        rel[0:69, :] = rel_ref[0:69, :].astype(F32)
-        rel[69:70, :] = rel_ref[64:65, :].astype(F32)
-        rel[70:71, :] = rel_ref[65:66, :].astype(F32)
-        wcat[:, 128:] = rel[...].T.astype(BF16)
-        for t in range(2):
-            up = wup_ref[t].astype(F32).T * gtrans_ref[t : t + 1, :]
-            wup[t, :256] = (up[:256] * 0.5).astype(BF16)
-            wup[t, 256:] = up[256:].astype(BF16)
-            wdn[t] = wdown_ref[t].astype(F32).T.astype(BF16)
-        wb[...] = (wbias_ref[...].astype(F32).T * gbias_ref[...]).astype(BF16)
-
+def prepare_bias(chain_k, res_k, refs, scratch):
+    gtrunk_ref, wpair_ref, rel_ref, gtrans_ref, wup_ref, wdown_ref, gbias_ref, wbias_ref = refs
+    low_ref, high_ref, wcat, wup, wdn, wb, rel = scratch
+    low, high = interval_bounds(chain_k, res_k)
+    low_ref[...] = low
+    high_ref[...] = high
+    wcat[:, :128] = (wpair_ref[...].astype(F32).T * gtrunk_ref[...]).astype(BF16)
+    rel[...] = jnp.zeros_like(rel)
+    rel[0:69, :] = rel_ref[0:69, :].astype(F32)
+    rel[69:70, :] = rel_ref[64:65, :].astype(F32)
+    rel[70:71, :] = rel_ref[65:66, :].astype(F32)
+    wcat[:, 128:] = rel[...].T.astype(BF16)
+    for t in range(2):
+        up = wup_ref[t].astype(F32).T * gtrans_ref[t : t + 1, :]
+        wup[t, :256] = (up[:256] * 0.5).astype(BF16)
+        wup[t, 256:] = up[256:].astype(BF16)
+        wdn[t] = wdown_ref[t].astype(F32).T.astype(BF16)
+    wb[...] = (wbias_ref[...].astype(F32) * gbias_ref[...]).astype(BF16)
+
+
+def bias_block(first, codes, z_ref, scratch, bias):
+    low_ref, high_ref, wcat, wup, wdn, wb, _ = scratch
     low = low_ref[...]
     high = high_ref[...]
-    tiles = [z_ref[j].astype(F32).T for j in range(QB)]
+    tiles = [z_ref[first + j].astype(F32).T for j in range(QB)]
     normed = norm_cols(jnp.concatenate(tiles, axis=1))
     hots = []
     for j in range(QB):
-        token = row_pos * 64 + step * QB + j
-        code = chain_sm[token] * 64 + res_sm[token]
+        code = codes(first + j)
         hots.append(jnp.where((low <= code) & (high >= code), 1.0, 0.0).astype(BF16))
     both = jnp.concatenate([normed, jnp.concatenate(hots, axis=1)], axis=0)
     pair = jnp.dot(wcat[...], both, preferred_element_type=F32)
@@ -89,43 +85,9 @@
         product = half * expanded[256:]
         swiglu = (product + product * jnp.tanh(half)).astype(BF16)
         pair = pair + jnp.dot(wdn[t], swiglu, preferred_element_type=F32)
-    bias = jnp.dot(wb[...], norm_cols(pair), preferred_element_type=F32)
+    out = jnp.dot(wb[...], norm_cols(pair), preferred_element_type=F32)
     for j in range(QB):
-        out_ref[j] = bias[:, j * 128 : (j + 1) * 128]
-
-
-def pair_bias(z, chain_id, residue, gain_trunk, w_pair, rel_table, gain_trans, w_up, w_down, gain_bias, w_bias):
-    def full(*shape):
-        return pl.BlockSpec(shape, lambda i, *_: (0,) * len(shape))
-
-    spec = pltpu.PrefetchScalarGridSpec(
-        num_scalar_prefetch=2,
-        grid=(64 // QB,),
-        in_specs=[
-            pl.BlockSpec((QB, 128, 128), lambda i, *_: (i, 0, 0)),
-            full(16, 128), full(16, 128), full(1, 128), full(128, 128), full(71, 128), full(2, 128),
-            full(2, 128, 512), full(2, 256, 128), full(1, 128), full(128, 16),
-        ],
-        out_specs=pl.BlockSpec((QB, 16, 128), lambda i, *_: (i, 0, 0)),
-        scratch_shapes=[
-            pltpu.VMEM((128, 128), jnp.int32),
-            pltpu.VMEM((128, 128), jnp.int32),
-            pltpu.VMEM((128, 256), BF16),
-            pltpu.VMEM((2, 512, 128), BF16),
-            pltpu.VMEM((2, 128, 256), BF16),
-            pltpu.VMEM((16, 128), BF16),
-            pltpu.VMEM((128, 128), F32),
-        ],
-    )
-    return pl.pallas_call(
-        bias_kernel,
-        grid_spec=spec,
-        out_shape=jax.ShapeDtypeStruct((64, 16, 128), F32),
-        compiler_params=pltpu.CompilerParams(vmem_limit_bytes=60 << 20),
-    )(
-        chain_id, residue, z, chain_id.reshape(16, 128), residue.reshape(16, 128), gain_trunk.reshape(1, 128),
-        w_pair, rel_table, gain_trans, w_up, w_down, gain_bias.reshape(1, 128), w_bias,
-    )
+        bias[pl.ds(pl.multiple_of((first + j) * 16, 16), 16), :] = out[:, j * 128 : (j + 1) * 128]
 
 
 def orders():
@@ -142,9 +104,11 @@
 
 
 def main_kernel(
-    x_ref, gain_ref, wt_ref, heads_ref, bias_hbm, wout_hbm, perm_hbm, out_ref,
+    chain_sm, res_sm, x_ref, gain_ref, wt_ref, heads_ref, chain_ref, res_ref,
+    gtrunk_ref, wpair_ref, rel_ref, gtrans_ref, wup_ref, wdown_ref, gbias_ref, wbias_ref,
+    z_hbm, wout_hbm, perm_hbm, out_ref,
     xs, xg, wg, xf, wf, kvs, qgs, kvz, kvb, qgb, tf, kt, vt, qf, gate, bias, wout, perm, woutp,
-    o_src, o_all, st_src, st_all, fac,
+    o_src, o_all, st_src, st_all, fac, zs, low, high, wcat, wup, wdn, wb, rel,
     local_sem, w_send, w_recv, x_send, x_recv, qg_send, qg_recv, kz_send, kz_recv, kv_send, kv_recv,
     o_send, o_recv, st_send, st_recv,
 ):
@@ -178,8 +142,9 @@
     def near(i):
         return lax.rem(16 + lax.div(i + 1, 2) * (1 - 2 * lax.rem(i, 2)), 16)
 
+
     loads = [
-        pltpu.make_async_copy(bias_hbm, bias, local_sem.at[0]),
+        pltpu.make_async_copy(z_hbm, zs, local_sem.at[0]),
         pltpu.make_async_copy(wout_hbm, wout, local_sem.at[1]),
         pltpu.make_async_copy(perm_hbm, perm, local_sem.at[2]),
     ]
@@ -199,12 +164,28 @@
     center = x - jnp.mean(x, axis=-1, keepdims=True)
     spread = jnp.mean(center * center, axis=-1, keepdims=True)
     xs[...] = (center * lax.rsqrt(spread + 1e-05) * gain_ref[...]).astype(BF16)
+    pair_scratch = (low, high, wcat, wup, wdn, wb, rel)
+    prepare_bias(
+        chain_ref[pl.ds(col_pos, 1), :], res_ref[pl.ds(col_pos, 1), :],
+        (gtrunk_ref, wpair_ref, rel_ref, gtrans_ref, wup_ref, wdown_ref, gbias_ref, wbias_ref), pair_scratch,
+    )
+
+    def code_of(index):
+        token = row_pos * 64 + index
+        return chain_sm[token] * 64 + res_sm[token]
+
+    def blocks(start, count):
+        loop(count, lambda i: bias_block((start + i) * QB, code_of, zs, pair_scratch, bias))
+
+    loads[0].wait()
+    blocks(0, B0)
     pl.semaphore_wait(barrier, 46)
 
     loop(15, lambda i: remote(wt_ref, wg.at[z], w_send, w_recv, line(lax.rem(z + far(i), 16))).start())
     loop(31, lambda i: remote(xs, xg.at[g], x_send, x_recv, plane(lax.rem(g + 1 + i, 32))).start())
     pltpu.make_async_copy(wt_ref, wg.at[z], w_recv).start()
     pltpu.make_async_copy(xs, xg.at[g], x_recv).start()
+    blocks(B0, B1)
     wait(xg, x_recv)
     for s in range(32):
         xf[4 * s : 4 * s + 4, :] = xg[s].astype(F32)
@@ -224,6 +205,7 @@
     pltpu.make_async_copy(kvs, kvz.at[z], kz_recv.at[z]).start()
     loads[1].wait()
     loads[2].wait()
+    blocks(B0 + B1, B2)
     woutp[...] = jnp.dot(perm[...], wout[...], preferred_element_type=F32).astype(BF16)
     wait(qgb, qg_recv)
 
@@ -244,6 +226,7 @@
     pick = jnp.where((rows + yh * 64 + col_pos * 4 == lanes) & (rows < 4), 1.0, 0.0).astype(BF16)
     gate[...] = lax.dot_general(pick, tf[...].astype(BF16), NT, preferred_element_type=F32)
 
+
     def forward(i):
         s = lax.rem(z + near(i), 16)
         wait(kvz.at[s], kz_recv.at[s])
@@ -259,7 +242,7 @@
                 remote(kvz.at[s], kvb.at[g], kv_send, kv_recv, {"row": z * 2 + y, "col": s}).start()
 
     loop(16, forward)
-    loads[0].wait()
+    blocks(B0 + B1 + B2, 64 // QB - B0 - B1 - B2)
     wait(kvb, kv_recv)
     unpack(kvb, 0, tf)
     kt[...] = tf[...].astype(BF16)
@@ -340,9 +323,6 @@
     z_trunk, chain_id, residue, single, gain_single, w_proj, w_out, gain_trunk, w_pair, rel_table, gain_trans,
     w_up, w_down, gain_bias, w_bias,
 ):
-    bias = pair_bias(
-        z_trunk, chain_id, residue, gain_trunk, w_pair, rel_table, gain_trans, w_up, w_down, gain_bias, w_bias
-    ).reshape(1024, 128)
     heads, perm = orders()
     vmem = pl.BlockSpec(memory_space=pltpu.VMEM)
     anywhere = pl.BlockSpec(memory_space=pl.ANY)
@@ -350,7 +330,7 @@
     return pl.pallas_call(
         main_kernel,
         out_shape=jax.ShapeDtypeStruct((4, 768), BF16),
-        in_specs=[vmem] * 4 + [anywhere] * 3,
+        in_specs=[pl.BlockSpec(memory_space=pltpu.SMEM)] * 2 + [vmem] * 14 + [anywhere] * 3,
         out_specs=vmem,
         scratch_shapes=[
             pltpu.VMEM((4, 768), BF16),
@@ -377,6 +357,14 @@
             pltpu.VMEM((16, 8, 128), F32),
             pltpu.VMEM((16, 8, 128), F32),
             pltpu.VMEM((64, 128), F32),
+            pltpu.VMEM((64, 128, 128), BF16),
+            pltpu.VMEM((128, 128), jnp.int32),
+            pltpu.VMEM((128, 128), jnp.int32),
+            pltpu.VMEM((128, 256), BF16),
+            pltpu.VMEM((2, 512, 128), BF16),
+            pltpu.VMEM((2, 128, 256), BF16),
+            pltpu.VMEM((16, 128), BF16),
+            pltpu.VMEM((128, 128), F32),
             dma((3,)),
             dma, dma, dma, dma, dma, dma, dma, dma((16,)), dma, dma, dma, dma, dma, dma,
         ],
@@ -384,8 +372,9 @@
             collective_id=0, has_side_effects=True, vmem_limit_bytes=40 << 20
         ),
     )(
-        single, gain_single.reshape(1, 768), w_proj.T, jnp.asarray(heads, BF16), bias, w_out,
-        jnp.asarray(perm, BF16),
+        chain_id, residue, single, gain_single.reshape(1, 768), w_proj.T, jnp.asarray(heads, BF16),
+        chain_id.reshape(16, 128), residue.reshape(16, 128), gain_trunk.reshape(1, 128), w_pair, rel_table, gain_trans,
+        w_up, w_down, gain_bias.reshape(1, 128), w_bias.T, z_trunk, w_out, jnp.asarray(perm, BF16),
     )
 
 

time: 70.8 us -> 70.3 us (level)
  Pallas kernels: 67.4 us -> 54.4 us
  local copies, waits for them, and re-layouts: 3.06 us -> 15.1 us
    pallas_call x1 -> x0, Pallas kernels: 13.9 us -> none  [pair_bias(): pl.pallas_call(bias_kernel, grid_spec=spec, out_shape=jax.ShapeDtypeStruc...]
    unnamed x16 -> x33, local copies, waits for them, and re-layouts: 3.06 us -> 14.4 us
    pallas_call x1, Pallas kernels: 53.5 us -> 54.4 us  [shards(): pl.pallas_call(main_kernel, out_shape=jax.ShapeDtypeStruct((4, 768), BF16...]
where the time goes in v2:
time: 70.3 us; the launch traced here: 69.6 us
  Pallas kernels  54.4 us (77%)
  local copies, waits for them, and re-layouts  15.1 us (21%)
    pallas_call x1, Pallas kernels, shards(): pl.pallas_call(main_kernel, out_shape=jax.ShapeDtypeStruct((4, 768), BF16...  54.4 us
    unnamed x33, local copies, waits for them, and re-layouts  14.4 us

profile of v2, /device:TPU:1, one launch (start us, length us, event | category | flops | bytes accessed | tf_op | source)
XLA Modules:
  0.0 69.6 jit_solution(9708458848707182943)
XLA Ops:
  0.0 0.7 reshape.15.gain_ref
  0.7 0.0 copy-start
  0.7 1.6 %copy-done = bf16[64,128,128]{2,1,0:T(8,128)(2,1)S(1)} copy-done((bf16[64,128,128]{2,1,0:T(8,128)(2,1)S(1)}, bf16[64,128,128]{2,1,0:T(8,128)(2,1)}, u32[]{:S(2)}) %copy-start) | copy-done | bytes 2097176
  2.3 0.0 copy-start.1
  2.3 1.3 %copy-done.1 = bf16[768,768]{1,0:T(8,128)(2,1)S(1)} copy-done((bf16[768,768]{1,0:T(8,128)(2,1)S(1)}, bf16[768,768]{1,0:T(8,128)(2,1)}, u32[]{:S(2)}) %copy-start.1) | copy-done | bytes 1179672
  3.6 0.0 copy-start.2
  3.6 1.3 %copy-done.2 = bf16[768,768]{1,0:T(8,128)(2,1)S(1)} copy-done((bf16[768,768]{1,0:T(8,128)(2,1)S(1)}, bf16[768,768]{1,0:T(8,128)(2,1)}, u32[]{:S(2)}) %copy-start.2) | copy-done | bytes 1179672
  4.8 0.0 copy-start.3
  4.8 0.9 %copy-done.3 = bf16[2,128,512]{2,1,0:T(8,128)(2,1)S(1)} copy-done((bf16[2,128,512]{2,1,0:T(8,128)(2,1)S(1)}, bf16[2,128,512]{2,1,0:T(8,128)(2,1)}, u32[]{:S(2)}) %copy-start.3) | copy-done | bytes 262168
  5.8 0.0 copy-start.4
  5.8 0.9 %copy-done.4 = bf16[128,768]{1,0:T(8,128)(2,1)S(1)} copy-done((bf16[128,768]{1,0:T(8,128)(2,1)S(1)}, bf16[128,768]{1,0:T(8,128)(2,1)}, u32[]{:S(2)}) %copy-start.4) | copy-done | bytes 196632
  6.7 0.9 %copy-done.5 = bf16[2,256,128]{2,1,0:T(8,128)(2,1)S(1)} copy-done((bf16[2,256,128]{2,1,0:T(8,128)(2,1)S(1)}, bf16[2,256,128]{2,1,0:T(8,128)(2,1)}, u32[]{:S(2)}) %copy-start.5) | copy-done | bytes 131096
  7.6 0.8 %copy-done.6 = bf16[128,128]{1,0:T(8,128)(2,1)S(1)} copy-done((bf16[128,128]{1,0:T(8,128)(2,1)S(1)}, bf16[128,128]{1,0:T(8,128)(2,1)}, u32[]{:S(2)}) %copy-start.6) | copy-done | bytes 32792
  8.4 0.7 copy-done.7
  9.1 0.7 copy-done.8
  9.8 0.7 %copy-done.9 = bf16[71,128]{1,0:T(8,128)(2,1)S(1)} copy-done((bf16[71,128]{1,0:T(8,128)(2,1)S(1)}, bf16[71,128]{1,0:T(8,128)(2,1)}, u32[]{:S(2)}) %copy-start.9) | copy-done | bytes 18200
  10.5 0.7 %copy-done.10 = bf16[768,6]{0,1:T(8,128)(2,1)S(1)} copy-done((bf16[768,6]{0,1:T(8,128)(2,1)S(1)}, bf16[768,6]{0,1:T(8,128)(2,1)}, u32[]{:S(2)}) %copy-start.10) | copy-done | bytes 9240
  11.2 0.7 copy-done.11
  11.9 0.7 copy-done.12
  12.6 0.7 copy-done.13
  13.3 0.7 copy-done.14
  13.9 0.7 copy-done.15
  14.6 54.4 %shard_map.163 = bf16[4,768]{1,0:T(4,128)(2,1)S(1)} custom-call(s32[2048]{0:T(1024)S(1)} %copy-done.7, s32[2048]{0:T(1024)S(1)} %copy-done.8, bf16[4,768]{1,0:T(4,128)(2,1)S(1)} %copy-done.11, f32[1,768]{1,0:T(1,128)S(1)} %reshape.15.gain_ref, bf16[6,768]{1,0:T(8,128)(2,1)S(1)} %bitcast.8, bf16[128,768]{1,0:T(8,128)(2,1)S(1)} %copy-done.4, ...), custom_call_target="tpu_custom_call" | custom-call | tf_op jit(solution)/shard_map/pallas_call | solution.py:330
  69.0 0.6 copy.19
  (11 shorter events, 0.0 us)
Async XLA Ops:
  0.7 1.6 %copy-start = (bf16[64,128,128]{2,1,0:T(8,128)(2,1)S(1)}, bf16[64,128,128]{2,1,0:T(8,128)(2,1)}, u32[]{:S(2)}) copy-start(bf16[64,128,128]{2,1,0:T(8,128)(2,1)} %z_hbm.1) | copy-start | bytes 6291460
  2.3 1.3 %copy-start.1 = (bf16[768,768]{1,0:T(8,128)(2,1)S(1)}, bf16[768,768]{1,0:T(8,128)(2,1)}, u32[]{:S(2)}) copy-start(bf16[768,768]{1,0:T(8,128)(2,1)} %wout_hbm.1) | copy-start | bytes 3538948
  3.6 1.3 %copy-start.2 = (bf16[768,768]{1,0:T(8,128)(2,1)S(1)}, bf16[768,768]{1,0:T(8,128)(2,1)}, u32[]{:S(2)}) copy-start(bf16[768,768]{1,0:T(8,128)(2,1)} %constant.5.clone.perm_hbm) | copy-start | bytes 3538948
  4.8 0.9 %copy-start.3 = (bf16[2,128,512]{2,1,0:T(8,128)(2,1)S(1)}, bf16[2,128,512]{2,1,0:T(8,128)(2,1)}, u32[]{:S(2)}) copy-start(bf16[2,128,512]{2,1,0:T(8,128)(2,1)} %wup_ref.1) | copy-start | bytes 786436
  5.8 0.9 %copy-start.4 = (bf16[128,768]{1,0:T(8,128)(2,1)S(1)}, bf16[128,768]{1,0:T(8,128)(2,1)}, u32[]{:S(2)}) copy-start(bf16[128,768]{1,0:T(8,128)(2,1)} %constant.4.clone.heads_ref) | copy-start | bytes 589828
  6.7 0.9 %copy-start.5 = (bf16[2,256,128]{2,1,0:T(8,128)(2,1)S(1)}, bf16[2,256,128]{2,1,0:T(8,128)(2,1)}, u32[]{:S(2)}) copy-start(bf16[2,256,128]{2,1,0:T(8,128)(2,1)} %wdown_ref.1) | copy-start | bytes 393220
  7.6 0.8 %copy-start.6 = (bf16[128,128]{1,0:T(8,128)(2,1)S(1)}, bf16[128,128]{1,0:T(8,128)(2,1)}, u32[]{:S(2)}) copy-start(bf16[128,128]{1,0:T(8,128)(2,1)} %wpair_ref.1) | copy-start | bytes 98308
  8.4 0.7 %copy-start.7 = (s32[2048]{0:T(1024)S(1)}, s32[2048]{0:T(1024)}, u32[]{:S(2)}) copy-start(s32[2048]{0:T(1024)} %chain_sm.1) | copy-start | bytes 24580
  9.1 0.7 %copy-start.8 = (s32[2048]{0:T(1024)S(1)}, s32[2048]{0:T(1024)}, u32[]{:S(2)}) copy-start(s32[2048]{0:T(1024)} %res_sm.1) | copy-start | bytes 24580
  9.8 0.7 %copy-start.9 = (bf16[71,128]{1,0:T(8,128)(2,1)S(1)}, bf16[71,128]{1,0:T(8,128)(2,1)}, u32[]{:S(2)}) copy-start(bf16[71,128]{1,0:T(8,128)(2,1)} %rel_ref.1) | copy-start | bytes 54532
  10.5 0.7 %copy-start.10 = (bf16[768,6]{0,1:T(8,128)(2,1)S(1)}, bf16[768,6]{0,1:T(8,128)(2,1)}, u32[]{:S(2)}) copy-start(bf16[768,6]{0,1:T(8,128)(2,1)} %param.22) | copy-start | bytes 27652
  11.2 0.7 copy-start.11
  11.9 0.7 copy-start.12
  12.6 0.7 copy-start.13
  13.2 0.7 copy-start.14
  13.9 0.7 copy-start.15

commit v3 on v2

--- a/solution.py
+++ b/solution.py
@@ -14,6 +14,8 @@
 BIG = 1 << 20
 QB = 16
 B0, B1, B2 = 1, 2, 1
+QA = 16
+OFFSETS = (2, 1, 3, 0)
 
 
 def norm_cols(values):
@@ -103,20 +105,29 @@
     return heads, perm
 
 
-def main_kernel(
-    chain_sm, res_sm, x_ref, gain_ref, wt_ref, heads_ref, chain_ref, res_ref,
-    gtrunk_ref, wpair_ref, rel_ref, gtrans_ref, wup_ref, wdown_ref, gbias_ref, wbias_ref,
-    z_hbm, wout_hbm, perm_hbm, out_ref,
-    xs, xg, wg, xf, wf, kvs, qgs, kvz, kvb, qgb, tf, kt, vt, qf, gate, bias, wout, perm, woutp,
-    o_src, o_all, st_src, st_all, fac, zs, low, high, wcat, wup, wdn, wb, rel,
-    local_sem, w_send, w_recv, x_send, x_recv, qg_send, qg_recv, kz_send, kz_recv, kv_send, kv_recv,
-    o_send, o_recv, st_send, st_recv,
-):
+HBM_ARGS = (
+    "x", "gain", "wt", "chain_sm", "res_sm", "chain", "res", "gtrunk", "wpair", "rel", "gtrans", "wup", "wdown", "gbias",
+    "wbias", "z", "heads", "wout", "perm",
+)
+
+
+def main_kernel(*refs):
+    count = len(HBM_ARGS)
+    source = dict(zip(HBM_ARGS, refs[:count]))
+    out_ref = refs[count]
+    held = dict(zip(HBM_ARGS, refs[count + 1 : 2 * count + 1]))
+    (
+        xs, xg, wg, xf, wf, kvs, qgs, kvz, kvb, qgb, kt, vt, qf, spread, gate, bias, woutp,
+        o_src, o_all, st_src, st_all, fac, low, high, wcat, wup, wdn, wb, rel,
+        local_sem, w_send, w_recv, x_send, x_recv, qg_send, qg_recv, kz_send, kz_recv, kv_send, kv_recv,
+        o_send, o_recv, st_send, st_recv,
+    ) = refs[2 * count + 1 :]
     row_pos = lax.axis_index("row")
     col_pos = lax.axis_index("col")
     z = lax.div(row_pos, 2)
     yh = lax.rem(row_pos, 2)
     g = yh * 16 + col_pos
+    middle = lax.rem(lax.div(z + 4, 8), 2)
 
     def line(zz):
         return {"row": zz * 2 + yh, "col": col_pos}
@@ -143,11 +154,10 @@
         return lax.rem(16 + lax.div(i + 1, 2) * (1 - 2 * lax.rem(i, 2)), 16)
 
 
-    loads = [
-        pltpu.make_async_copy(z_hbm, zs, local_sem.at[0]),
-        pltpu.make_async_copy(wout_hbm, wout, local_sem.at[1]),
-        pltpu.make_async_copy(perm_hbm, perm, local_sem.at[2]),
-    ]
+    loads = {
+        name: pltpu.make_async_copy(source[name], held[name], local_sem.at[index])
+        for index, name in enumerate(HBM_ARGS)
+    }
     barrier = pltpu.get_barrier_semaphore()
 
     def greet_line(i):
@@ -158,73 +168,87 @@
 
     loop(15, greet_line)
     loop(31, greet_plane)
-    for load in loads:
-        load.start()
-    x = x_ref[...].astype(F32)
+    for name in HBM_ARGS:
+        loads[name].start()
+    loads["x"].wait()
+    loads["gain"].wait()
+    x = held["x"][...].astype(F32)
     center = x - jnp.mean(x, axis=-1, keepdims=True)
-    spread = jnp.mean(center * center, axis=-1, keepdims=True)
-    xs[...] = (center * lax.rsqrt(spread + 1e-05) * gain_ref[...]).astype(BF16)
+    deviation = jnp.mean(center * center, axis=-1, keepdims=True)
+    gain = jnp.concatenate([held["gain"][k : k + 1, :] for k in range(6)], axis=1)
+    xs[...] = (center * lax.rsqrt(deviation + 1e-05) * gain).astype(BF16)
+    pair_args = ("gtrunk", "wpair", "rel", "gtrans", "wup", "wdown", "gbias", "wbias")
+    for name in ("wt", "heads", "chain", "res", "chain_sm", "res_sm", "z") + pair_args:
+        loads[name].wait()
     pair_scratch = (low, high, wcat, wup, wdn, wb, rel)
     prepare_bias(
-        chain_ref[pl.ds(col_pos, 1), :], res_ref[pl.ds(col_pos, 1), :],
-        (gtrunk_ref, wpair_ref, rel_ref, gtrans_ref, wup_ref, wdown_ref, gbias_ref, wbias_ref), pair_scratch,
+        held["chain"][pl.ds(col_pos, 1), :], held["res"][pl.ds(col_pos, 1), :],
+        [held[name] for name in pair_args], pair_scratch,
     )
 
     def code_of(index):
         token = row_pos * 64 + index
-        return chain_sm[token] * 64 + res_sm[token]
+        return held["chain_sm"][token] * 64 + held["res_sm"][token]
 
     def blocks(start, count):
-        loop(count, lambda i: bias_block((start + i) * QB, code_of, zs, pair_scratch, bias))
-
-    loads[0].wait()
+        loop(count, lambda i: bias_block((start + i) * QB, code_of, held["z"], pair_scratch, bias))
+
     blocks(0, B0)
     pl.semaphore_wait(barrier, 46)
 
-    loop(15, lambda i: remote(wt_ref, wg.at[z], w_send, w_recv, line(lax.rem(z + far(i), 16))).start())
+    wt = held["wt"]
+    loop(15, lambda i: remote(wt, wg.at[z], w_send, w_recv.at[middle], line(lax.rem(z + far(i), 16))).start())
     loop(31, lambda i: remote(xs, xg.at[g], x_send, x_recv, plane(lax.rem(g + 1 + i, 32))).start())
-    pltpu.make_async_copy(wt_ref, wg.at[z], w_recv).start()
+    pltpu.make_async_copy(wt, wg.at[z], w_recv.at[middle]).start()
     pltpu.make_async_copy(xs, xg.at[g], x_recv).start()
     blocks(B0, B1)
     wait(xg, x_recv)
     for s in range(32):
         xf[4 * s : 4 * s + 4, :] = xg[s].astype(F32)
-    wait(wg, w_recv)
-    for s in range(16):
-        wf[6 * s : 6 * s + 6, :] = wg[s].astype(F32)
+    tokens = xf[...].astype(BF16)
+    wait(wg.at[pl.ds(4, 8)], w_recv.at[1])
+    for s in range(8):
+        wf[6 * s : 6 * s + 6, :] = wg[4 + s].astype(F32)
+    kvs[...] = lax.dot_general(wf[...].astype(BF16), tokens, NT, preferred_element_type=F32).astype(BF16)
+
+    loop(15, lambda i: remote(kvs, kvz.at[z], kz_send, kz_recv.at[z], line(lax.rem(z + far(i), 16))).start())
+    pltpu.make_async_copy(kvs, kvz.at[z], kz_recv.at[z]).start()
+    loads["wout"].wait()
+    loads["perm"].wait()
+    woutp[...] = jnp.dot(held["perm"][...], held["wout"][...], preferred_element_type=F32).astype(BF16)
+    wait(wg.at[pl.ds(0, 8)], w_recv.at[0])
+    for s in range(8):
+        wf[6 * s : 6 * s + 6, :] = wg[s if s < 4 else s + 8].astype(F32)
     projected = lax.dot_general(
         wf[...].astype(BF16), xf[...].astype(BF16), NT, preferred_element_type=F32
     )
-    kvs[...] = projected[24:72].astype(BF16)
     qgs[0:24] = projected[0:24].astype(BF16)
-    qgs[24:48] = jax.nn.sigmoid(projected[72:96]).astype(BF16)
-
-    loop(15, lambda i: remote(kvs, kvz.at[z], kz_send, kz_recv.at[z], line(lax.rem(z + far(i), 16))).start())
+    qgs[24:48] = jax.nn.sigmoid(projected[24:48]).astype(BF16)
     loop(31, lambda i: remote(qgs, qgb.at[g], qg_send, qg_recv, plane(lax.rem(g + 1 + i, 32))).start())
     pltpu.make_async_copy(qgs, qgb.at[g], qg_recv).start()
-    pltpu.make_async_copy(kvs, kvz.at[z], kz_recv.at[z]).start()
-    loads[1].wait()
-    loads[2].wait()
     blocks(B0 + B1, B2)
-    woutp[...] = jnp.dot(perm[...], wout[...], preferred_element_type=F32).astype(BF16)
     wait(qgb, qg_recv)
 
-    def unpack(ref, first, dst):
-        def body(s):
-            dst[pl.ds(pl.multiple_of(s * 24, 8), 24), :] = ref[s, first : first + 24, :].astype(F32)
-
-        loop(32, body)
-
-    unpack(qgb, 0, tf)
+    def unpack(ref, first):
+        return ref[:, first : first + 24, :].astype(F32).reshape(768, 128).astype(BF16)
+
     rows = lax.broadcasted_iota(jnp.int32, (64, 128), 0)
     lanes = lax.broadcasted_iota(jnp.int32, (64, 128), 1)
     pick = jnp.where(rows + yh * 64 == lanes, 1.0, 0.0).astype(BF16)
-    qf[...] = lax.dot_general(pick, tf[...].astype(BF16), NT, preferred_element_type=F32)
-    unpack(qgb, 24, tf)
+    qf[...] = lax.dot_general(pick, unpack(qgb, 0), NT, preferred_element_type=F32)
+    mask = held["heads"][0:16, :].astype(F32)
+
+    def spread_queries(i):
+        queries = qf[pl.ds(pl.multiple_of(i * 8, 8), 8), :]
+        spread[pl.ds(pl.multiple_of(i * 128, 128), 128), :] = (
+            (queries[:, None, :] * mask[None]).reshape(128, 768).astype(BF16)
+        )
+
+    loop(8, spread_queries)
     rows = lax.broadcasted_iota(jnp.int32, (8, 128), 0)
     lanes = lax.broadcasted_iota(jnp.int32, (8, 128), 1)
     pick = jnp.where((rows + yh * 64 + col_pos * 4 == lanes) & (rows < 4), 1.0, 0.0).astype(BF16)
-    gate[...] = lax.dot_general(pick, tf[...].astype(BF16), NT, preferred_element_type=F32)
+    gate[...] = lax.dot_general(pick, unpack(qgb, 24), NT, preferred_element_type=F32)
 
 
     def forward(i):
@@ -244,14 +268,10 @@
     loop(16, forward)
     blocks(B0 + B1 + B2, 64 // QB - B0 - B1 - B2)
     wait(kvb, kv_recv)
-    unpack(kvb, 0, tf)
-    kt[...] = tf[...].astype(BF16)
-    unpack(kvb, 24, tf)
-    vt[...] = tf[...].astype(BF16)
-
-    mask = heads_ref[0:16, :].astype(F32)
-    rows = lax.broadcasted_iota(jnp.int32, (128, 128), 0)
-    lanes = lax.broadcasted_iota(jnp.int32, (128, 128), 1)
+    kt[...] = unpack(kvb, 0)
+    vt[...] = unpack(kvb, 24)
+    rows = lax.broadcasted_iota(jnp.int32, (QA * 16, 128), 0)
+    lanes = lax.broadcasted_iota(jnp.int32, (QA * 16, 128), 1)
     own = jnp.where(jnp.bitwise_and(rows, 15) == lanes, 1.0, 0.0)
 
     def send_parts(d):
@@ -267,24 +287,28 @@
             remote(st_src.at[d], st_all.at[col_pos], st_send, st_recv, there).start()
 
     def attend(i):
-        base = pl.multiple_of(i * 128, 128)
-        queries = qf[pl.ds(pl.multiple_of(i * 8, 8), 8), :]
-        spread_q = (queries[:, None, :] * mask[None]).reshape(128, 768).astype(BF16)
-        scores = jnp.dot(spread_q, kt[...], preferred_element_type=F32) * (48.0**-0.5) + bias[pl.ds(base, 128), :]
+        base = pl.multiple_of(i * (QA * 16), QA * 16)
+        scores = jnp.dot(spread[pl.ds(base, QA * 16), :], kt[...], preferred_element_type=F32)
+        scores = scores * (48.0**-0.5) + bias[pl.ds(base, QA * 16), :]
         peak = jnp.max(scores, axis=-1, keepdims=True)
         expo = jnp.exp(scores - peak)
         total = jnp.sum(expo, axis=-1, keepdims=True)
         wide = lax.dot_general(expo.astype(BF16), vt[...], NT, preferred_element_type=F32)
-        summed = jnp.sum(wide.reshape(8, 16, 768) * mask[None], axis=1).astype(BF16)
-        peaks = jnp.sum((peak * own).reshape(8, 16, 128), axis=1)
-        totals = jnp.sum((total * own).reshape(8, 16, 128), axis=1)
-        for k in range(2):
-            o_src[i * 2 + k] = summed[4 * k : 4 * k + 4]
-            st_src[i * 2 + k, 0:4, :] = peaks[4 * k : 4 * k + 4]
-            st_src[i * 2 + k, 4:8, :] = totals[4 * k : 4 * k + 4]
-
-    loop(8, attend)
-    loop(16, send_parts)
+        summed = jnp.sum(wide.reshape(QA, 16, 768) * mask[None], axis=1).astype(BF16)
+        peaks = jnp.sum((peak * own).reshape(QA, 16, 128), axis=1)
+        totals = jnp.sum((total * own).reshape(QA, 16, 128), axis=1)
+        for k in range(QA // 4):
+            part = i * (QA // 4) + k
+            o_src[part] = summed[4 * k : 4 * k + 4]
+            st_src[part, 0:4, :] = peaks[4 * k : 4 * k + 4]
+            st_src[part, 4:8, :] = totals[4 * k : 4 * k + 4]
+
+    parts = 64 // QA
+    first = lax.div(col_pos, QA // 4)
+    for offset in OFFSETS:
+        block = lax.rem(first + offset, parts)
+        attend(block)
+        loop(QA // 4, lambda k, block=block: send_parts(block * (QA // 4) + k))
     wait(st_all, st_recv)
     stats = st_all[...]
     peak = stats[0, 0:4]
@@ -300,8 +324,8 @@
         fac[4 * s : 4 * s + 4, :] = jnp.where(lanes < 16, factors[s] * inverse, 0.0)
     coarse = fac[...].astype(BF16)
     fine = (fac[...] - coarse.astype(F32)).astype(BF16)
-    wide = jnp.dot(coarse, heads_ref[...], preferred_element_type=F32) + jnp.dot(
-        fine, heads_ref[...], preferred_element_type=F32
+    wide = jnp.dot(coarse, held["heads"][...], preferred_element_type=F32) + jnp.dot(
+        fine, held["heads"][...], preferred_element_type=F32
     )
     wait(o_all, o_recv)
     summed = wide[0:4] * o_all[0].astype(F32)
@@ -324,40 +348,60 @@
     w_up, w_down, gain_bias, w_bias,
 ):
     heads, perm = orders()
-    vmem = pl.BlockSpec(memory_space=pltpu.VMEM)
-    anywhere = pl.BlockSpec(memory_space=pl.ANY)
     dma = pltpu.SemaphoreType.DMA
+    args = {
+        "x": single,
+        "gain": gain_single.reshape(6, 128),
+        "wt": w_proj.T,
+        "heads": jnp.asarray(heads, BF16),
+        "chain": chain_id.reshape(16, 128),
+        "res": residue.reshape(16, 128),
+        "gtrunk": gain_trunk.reshape(1, 128),
+        "wpair": w_pair,
+        "rel": rel_table,
+        "gtrans": gain_trans,
+        "wup": w_up,
+        "wdown": w_down,
+        "gbias": gain_bias.reshape(1, 128),
+        "wbias": w_bias.T,
+        "wout": w_out,
+        "perm": jnp.asarray(perm, BF16),
+        "z": z_trunk,
+        "chain_sm": chain_id,
+        "res_sm": residue,
+    }
+    held = [
+        (pltpu.SMEM if name.endswith("_sm") else pltpu.VMEM)(args[name].shape, args[name].dtype) for name in HBM_ARGS
+    ]
     return pl.pallas_call(
         main_kernel,
         out_shape=jax.ShapeDtypeStruct((4, 768), BF16),
-        in_specs=[pl.BlockSpec(memory_space=pltpu.SMEM)] * 2 + [vmem] * 14 + [anywhere] * 3,
-        out_specs=vmem,
-        scratch_shapes=[
+        in_specs=[pl.BlockSpec(memory_space=pltpu.HBM)] * len(HBM_ARGS),
+        out_specs=pl.BlockSpec(memory_space=pltpu.VMEM),
+        scratch_shapes=held
+        + [
             pltpu.VMEM((4, 768), BF16),
             pltpu.VMEM((32, 4, 768), BF16),
             pltpu.VMEM((16, 6, 768), BF16),
             pltpu.VMEM((128, 768), F32),
-            pltpu.VMEM((96, 768), F32),
+            pltpu.VMEM((48, 768), F32),
             pltpu.VMEM((48, 128), BF16),
             pltpu.VMEM((48, 128), BF16),
             pltpu.VMEM((16, 48, 128), BF16),
             pltpu.VMEM((32, 48, 128), BF16),
             pltpu.VMEM((32, 48, 128), BF16),
-            pltpu.VMEM((768, 128), F32),
             pltpu.VMEM((768, 128), BF16),
             pltpu.VMEM((768, 128), BF16),
             pltpu.VMEM((64, 768), F32),
+            pltpu.VMEM((1024, 768), BF16),
             pltpu.VMEM((8, 768), F32),
             pltpu.VMEM((1024, 128), F32),
-            pltpu.VMEM((768, 768), BF16),
-            pltpu.VMEM((768, 768), BF16),
             pltpu.VMEM((768, 768), BF16),
             pltpu.VMEM((16, 4, 768), BF16),
             pltpu.VMEM((16, 4, 768), BF16),
             pltpu.VMEM((16, 8, 128), F32),
             pltpu.VMEM((16, 8, 128), F32),
             pltpu.VMEM((64, 128), F32),
-            pltpu.VMEM((64, 128, 128), BF16),
             pltpu.VMEM((128, 128), jnp.int32),
             pltpu.VMEM((128, 128), jnp.int32),
             pltpu.VMEM((128, 256), BF16),
@@ -365,17 +409,13 @@
             pltpu.VMEM((2, 128, 256), BF16),
             pltpu.VMEM((16, 128), BF16),
             pltpu.VMEM((128, 128), F32),
-            dma((3,)),
-            dma, dma, dma, dma, dma, dma, dma, dma((16,)), dma, dma, dma, dma, dma, dma,
+            dma((len(HBM_ARGS),)),
+            dma, dma((2,)), dma, dma, dma, dma, dma, dma((16,)), dma, dma, dma, dma, dma, dma,
         ],
         compiler_params=pltpu.CompilerParams(
-            collective_id=0, has_side_effects=True, vmem_limit_bytes=40 << 20
+            collective_id=0, has_side_effects=True, vmem_limit_bytes=67043328
         ),
-    )(
-        chain_id, residue, single, gain_single.reshape(1, 768), w_proj.T, jnp.asarray(heads, BF16),
-        chain_id.reshape(16, 128), residue.reshape(16, 128), gain_trunk.reshape(1, 128), w_pair, rel_table, gain_trans,
-        w_up, w_down, gain_bias.reshape(1, 128), w_bias.T, z_trunk, w_out, jnp.asarray(perm, BF16),
-    )
+    )(*[args[name] for name in HBM_ARGS])
 
 
 def solution(mesh):

time: 70.3 us -> 54.1 us (0.77)
  local copies, waits for them, and re-layouts: 15.1 us -> 1.29 us
  Pallas kernels: 54.4 us -> 52.6 us
    unnamed x33 -> x1, local copies, waits for them, and re-layouts: 14.4 us -> 1.29 us
    pallas_call x1, Pallas kernels: 54.4 us -> 52.6 us  [shards(): pl.pallas_call(main_kernel, out_shape=jax.ShapeDtypeStruct((4, 768), BF16...]
where the time goes in v3:
time: 54.1 us; the launch traced here: 53.9 us
  Pallas kernels  52.6 us (97%)
  local copies, waits for them, and re-layouts  1.29 us (2%)
    pallas_call x1, Pallas kernels, shards(): pl.pallas_call(main_kernel, out_shape=jax.ShapeDtypeStruct((4, 768), BF16...  52.6 us
    unnamed x1, local copies, waits for them, and re-layouts  1.29 us

profile of v3, /device:TPU:1, one launch (start us, length us, event | category | flops | bytes accessed | tf_op | source)
XLA Modules:
  0.0 53.9 jit_solution(15117163438058170568)
XLA Ops:
  0.0 52.6 %shard_map.163 = bf16[4,768]{1,0:T(4,128)(2,1)} custom-call(bf16[4,768]{1,0:T(4,128)(2,1)} %refs_0_.1, f32[6,128]{1,0:T(8,128)} %bitcast.10, bf16[6,768]{1,0:T(8,128)(2,1)} %bitcast.9, s32[2048]{0:T(1024)} %refs_3_.1, s32[2048]{0:T(1024)} %refs_4_.1, s32[16,128]{1,0:T(8,128)} %bitcast.7, s32[16,128]{1,0:T(8,128)} %bitcast.8, f32[1,128]{1,0:T(1,128)} %bitcast.12, ...), custom_call_target="tpu_custom_call" | custom-call | tf_op jit(solution)/shard_map/pallas_call | solution.py:376
  52.6 1.3 %copy.19 = bf16[4,768]{1,0:T(4,128)(2,1)} copy(bf16[4,768]{1,0:T(4,128)(2,1)} %shard_map.163) | data formatting | bytes 12288

commit v4 on v3

--- a/solution.py
+++ b/solution.py
@@ -13,9 +13,8 @@
 BF16 = jnp.bfloat16
 BIG = 1 << 20
 QB = 16
-B0, B1, B2 = 1, 2, 1
-QA = 16
-OFFSETS = (2, 1, 3, 0)
+QA = 32
+OFFSETS = (1, 0)
 
 
 def norm_cols(values):
@@ -193,7 +192,9 @@
     def blocks(start, count):
         loop(count, lambda i: bias_block((start + i) * QB, code_of, held["z"], pair_scratch, bias))
 
-    blocks(0, B0)
+    ahead = jnp.where(z < 4, 3, jnp.where(z < 8, 1, 0))
+    meanwhile = jnp.where(z < 4, 1, 2)
+    blocks(0, ahead)
     pl.semaphore_wait(barrier, 46)
 
     wt = held["wt"]
@@ -201,7 +202,10 @@
     loop(31, lambda i: remote(xs, xg.at[g], x_send, x_recv, plane(lax.rem(g + 1 + i, 32))).start())
     pltpu.make_async_copy(wt, wg.at[z], w_recv.at[middle]).start()
     pltpu.make_async_copy(xs, xg.at[g], x_recv).start()
-    blocks(B0, B1)
+    blocks(ahead, meanwhile)
+    loads["wout"].wait()
+    loads["perm"].wait()
+    woutp[...] = jnp.dot(held["perm"][...], held["wout"][...], preferred_element_type=F32).astype(BF16)
     wait(xg, x_recv)
     for s in range(32):
         xf[4 * s : 4 * s + 4, :] = xg[s].astype(F32)
@@ -213,9 +217,6 @@
 
     loop(15, lambda i: remote(kvs, kvz.at[z], kz_send, kz_recv.at[z], line(lax.rem(z + far(i), 16))).start())
     pltpu.make_async_copy(kvs, kvz.at[z], kz_recv.at[z]).start()
-    loads["wout"].wait()
-    loads["perm"].wait()
-    woutp[...] = jnp.dot(held["perm"][...], held["wout"][...], preferred_element_type=F32).astype(BF16)
     wait(wg.at[pl.ds(0, 8)], w_recv.at[0])
     for s in range(8):
         wf[6 * s : 6 * s + 6, :] = wg[s if s < 4 else s + 8].astype(F32)
@@ -226,7 +227,22 @@
     qgs[24:48] = jax.nn.sigmoid(projected[24:48]).astype(BF16)
     loop(31, lambda i: remote(qgs, qgb.at[g], qg_send, qg_recv, plane(lax.rem(g + 1 + i, 32))).start())
     pltpu.make_async_copy(qgs, qgb.at[g], qg_recv).start()
-    blocks(B0 + B1, B2)
+    def forward(i):
+        s = lax.rem(z + near(i), 16)
+        wait(kvz.at[s], kz_recv.at[s])
+        for y in range(2):
+            itself = (yh == y) & (col_pos == s)
+
+            @pl.when(itself)
+            def _():
+                pltpu.make_async_copy(kvz.at[s], kvb.at[g], kv_recv).start()
+
+            @pl.when(jnp.logical_not(itself))
+            def _():
+                remote(kvz.at[s], kvb.at[g], kv_send, kv_recv, {"row": z * 2 + y, "col": s}).start()
+
+    loop(8, forward)
+    blocks(ahead + meanwhile, 64 // QB - ahead - meanwhile)
     wait(qgb, qg_recv)
 
     def unpack(ref, first):
@@ -251,22 +267,7 @@
     gate[...] = lax.dot_general(pick, unpack(qgb, 24), NT, preferred_element_type=F32)
 
 
-    def forward(i):
-        s = lax.rem(z + near(i), 16)
-        wait(kvz.at[s], kz_recv.at[s])
-        for y in range(2):
-            itself = (yh == y) & (col_pos == s)
-
-            @pl.when(itself)
-            def _():
-                pltpu.make_async_copy(kvz.at[s], kvb.at[g], kv_recv).start()
-
-            @pl.when(jnp.logical_not(itself))
-            def _():
-                remote(kvz.at[s], kvb.at[g], kv_send, kv_recv, {"row": z * 2 + y, "col": s}).start()
-
-    loop(16, forward)
-    blocks(B0 + B1 + B2, 64 // QB - B0 - B1 - B2)
+    loop(8, lambda i: forward(i + 8))
     wait(kvb, kv_recv)
     kt[...] = unpack(kvb, 0)
     vt[...] = unpack(kvb, 24)

time: 54.1 us -> 52.5 us (0.970)
  Pallas kernels: 52.6 us -> 50.9 us
    pallas_call x1, Pallas kernels: 52.6 us -> 50.9 us  [shards(): pl.pallas_call(main_kernel, out_shape=jax.ShapeDtypeStruct((4, 768), BF16...]
where the time goes in v4:
time: 52.5 us; the launch traced here: 52.2 us
  Pallas kernels  50.9 us (97%)
  local copies, waits for them, and re-layouts  1.29 us (2%)
    pallas_call x1, Pallas kernels, shards(): pl.pallas_call(main_kernel, out_shape=jax.ShapeDtypeStruct((4, 768), BF16...  50.9 us
    unnamed x1, local copies, waits for them, and re-layouts  1.29 us

profile of v4, /device:TPU:1, one launch (start us, length us, event | category | flops | bytes accessed | tf_op | source)
XLA Modules:
  0.0 52.2 jit_solution(11652162932669323259)
XLA Ops:
  0.0 50.9 %shard_map.163 = bf16[4,768]{1,0:T(4,128)(2,1)} custom-call(bf16[4,768]{1,0:T(4,128)(2,1)} %refs_0_.1, f32[6,128]{1,0:T(8,128)} %bitcast.10, bf16[6,768]{1,0:T(8,128)(2,1)} %bitcast.9, s32[2048]{0:T(1024)} %refs_3_.1, s32[2048]{0:T(1024)} %refs_4_.1, s32[16,128]{1,0:T(8,128)} %bitcast.7, s32[16,128]{1,0:T(8,128)} %bitcast.8, f32[1,128]{1,0:T(1,128)} %bitcast.12, ...), custom_call_target="tpu_custom_call" | custom-call | tf_op jit(solution)/shard_map/pallas_call | solution.py:377
  51.0 1.3 %copy.19 = bf16[4,768]{1,0:T(4,128)(2,1)} copy(bf16[4,768]{1,0:T(4,128)(2,1)} %shard_map.163) | data formatting | bytes 12288

commit v5 on v4

--- a/solution.py
+++ b/solution.py
@@ -275,17 +275,14 @@
     lanes = lax.broadcasted_iota(jnp.int32, (QA * 16, 128), 1)
     own = jnp.where(jnp.bitwise_and(rows, 15) == lanes, 1.0, 0.0)
 
-    def send_parts(d):
+    def send_part(src, dst, send, recv, d):
         @pl.when(d == col_pos)
         def _():
-            pltpu.make_async_copy(o_src.at[d], o_all.at[col_pos], o_recv).start()
-            pltpu.make_async_copy(st_src.at[d], st_all.at[col_pos], st_recv).start()
+            pltpu.make_async_copy(src.at[d], dst.at[col_pos], recv).start()
 
         @pl.when(d != col_pos)
         def _():
-            there = {"row": row_pos, "col": d}
-            remote(o_src.at[d], o_all.at[col_pos], o_send, o_recv, there).start()
-            remote(st_src.at[d], st_all.at[col_pos], st_send, st_recv, there).start()
+            remote(src.at[d], dst.at[col_pos], send, recv, {"row": row_pos, "col": d}).start()
 
     def attend(i):
         base = pl.multiple_of(i * (QA * 16), QA * 16)
@@ -294,22 +291,23 @@
         peak = jnp.max(scores, axis=-1, keepdims=True)
         expo = jnp.exp(scores - peak)
         total = jnp.sum(expo, axis=-1, keepdims=True)
-        wide = lax.dot_general(expo.astype(BF16), vt[...], NT, preferred_element_type=F32)
-        summed = jnp.sum(wide.reshape(QA, 16, 768) * mask[None], axis=1).astype(BF16)
         peaks = jnp.sum((peak * own).reshape(QA, 16, 128), axis=1)
         totals = jnp.sum((total * own).reshape(QA, 16, 128), axis=1)
         for k in range(QA // 4):
             part = i * (QA // 4) + k
-            o_src[part] = summed[4 * k : 4 * k + 4]
             st_src[part, 0:4, :] = peaks[4 * k : 4 * k + 4]
             st_src[part, 4:8, :] = totals[4 * k : 4 * k + 4]
+        loop(QA // 4, lambda k: send_part(st_src, st_all, st_send, st_recv, i * (QA // 4) + k))
+        wide = lax.dot_general(expo.astype(BF16), vt[...], NT, preferred_element_type=F32)
+        summed = jnp.sum(wide.reshape(QA, 16, 768) * mask[None], axis=1).astype(BF16)
+        for k in range(QA // 4):
+            o_src[i * (QA // 4) + k] = summed[4 * k : 4 * k + 4]
+        loop(QA // 4, lambda k: send_part(o_src, o_all, o_send, o_recv, i * (QA // 4) + k))
 
     parts = 64 // QA
     first = lax.div(col_pos, QA // 4)
     for offset in OFFSETS:
-        block = lax.rem(first + offset, parts)
-        attend(block)
-        loop(QA // 4, lambda k, block=block: send_parts(block * (QA // 4) + k))
+        attend(lax.rem(first + offset, parts))
     wait(st_all, st_recv)
     stats = st_all[...]
     peak = stats[0, 0:4]

time: 52.5 us -> 52.8 us (level)
  no operation moved by 1% of the time
where the time goes in v5:
time: 52.8 us; the launch traced here: 52.6 us
  Pallas kernels  51.3 us (97%)
  local copies, waits for them, and re-layouts  1.29 us (2%)
    pallas_call x1, Pallas kernels, shards(): pl.pallas_call(main_kernel, out_shape=jax.ShapeDtypeStruct((4, 768), BF16...  51.3 us
    unnamed x1, local copies, waits for them, and re-layouts  1.29 us

profile of v5, /device:TPU:1, one launch (start us, length us, event | category | flops | bytes accessed | tf_op | source)
XLA Modules:
  0.0 52.6 jit_solution(2333709276661891575)
XLA Ops:
  0.0 51.3 %shard_map.163 = bf16[4,768]{1,0:T(4,128)(2,1)} custom-call(bf16[4,768]{1,0:T(4,128)(2,1)} %refs_0_.1, f32[6,128]{1,0:T(8,128)} %bitcast.10, bf16[6,768]{1,0:T(8,128)(2,1)} %bitcast.9, s32[2048]{0:T(1024)} %refs_3_.1, s32[2048]{0:T(1024)} %refs_4_.1, s32[16,128]{1,0:T(8,128)} %bitcast.7, s32[16,128]{1,0:T(8,128)} %bitcast.8, f32[1,128]{1,0:T(1,128)} %bitcast.12, ...), custom_call_target="tpu_custom_call" | custom-call | tf_op jit(solution)/shard_map/pallas_call | solution.py:375
  51.3 1.3 %copy.19 = bf16[4,768]{1,0:T(4,128)(2,1)} copy(bf16[4,768]{1,0:T(4,128)(2,1)} %shard_map.163) | data formatting | bytes 12288
